TPU v7x, 32 devices: a whole 2x2x4 slice. The times are simulated.
32 devices in a mesh: row: 4 (over z), col: 8 (over y, x, core).
Axes of the slice: x: 2, y: 2, z: 4, core: 2. Of those that a mesh axis runs over, the one named last changes fastest.
Arguments:
- tokens: bfloat16 [8192, 2048], P('row', 'col'), may hold values from -6 to 6
- doc_ids: int32 [8192], P('row'), may hold values from 0 to 15, never falling along the last dimension, each value on 1 to 1024 neighbouring positions
- norm1_gain: bfloat16 [2048], P('col'), may hold values from 0.5 to 1.5
- norm1_bias: bfloat16 [2048], P('col'), may hold values from -1.796875 to 1.796875
- norm2_gain: bfloat16 [2048], P('col'), may hold values from 0.5 to 1.5
- norm2_bias: bfloat16 [2048], P('col'), may hold values from -1.796875 to 1.796875
- w_qkv: bfloat16 [2048, 16, 384], P('row', 'col'), may hold values from -0.125 to 0.125
- b_qkv: bfloat16 [16, 384], P('col'), may hold values from -1.796875 to 1.796875
- w_out: bfloat16 [2048, 2048], P('col', 'row'), may hold values from -0.5 to 0.5
- b_out: bfloat16 [2048], P('row'), may hold values from -1.796875 to 1.796875
- w_up: bfloat16 [2048, 8192], P('row', 'col'), may hold values from -0.125 to 0.125
- b_up: bfloat16 [8192], P('col'), may hold values from -1.796875 to 1.796875
- w_down: bfloat16 [8192, 2048], P('col', 'row'), may hold values from -0.0625 to 0.0625
- b_down: bfloat16 [2048], P('row'), may hold values from -1.796875 to 1.796875
- cotangent: bfloat16 [8192, 2048], P('row', 'col'), may hold values from -6 to 6
Outputs:
- layer_out: bfloat16 [8192, 2048], P('row', 'col')
- grad_tokens: float32 [8192, 2048], P('row', 'col')
- grad_norm1_gain: float32 [2048], P('col')
- grad_norm1_bias: float32 [2048], P('col')
- grad_norm2_gain: float32 [2048], P('col')
- grad_norm2_bias: float32 [2048], P('col')
- grad_w_qkv: float32 [2048, 16, 384], P('row', 'col')
- grad_b_qkv: float32 [16, 384], P('col')
- grad_w_out: float32 [2048, 2048], P('col', 'row')
- grad_b_out: float32 [2048], P('row')
- grad_w_up: float32 [2048, 8192], P('row', 'col')
- grad_b_up: float32 [8192], P('col')
- grad_w_down: float32 [8192, 2048], P('col', 'row')
- grad_b_down: float32 [2048], P('row')
Inputs may be any that keep to these rules, and one draw needn't show every extreme that they name: `doc_ids`: document numbers never fall along the tokens.
All inputs are finite; a program needn't handle non-finite values.
Results may differ from a plain program's by a relative error of at most 0.0095.
Values may be sent and summed in bfloat16 or wider, within the bound.
No kernel may reach another device: no remote copies, remote signals or barrier semaphores. Data moves between devices by JAX's collectives and lax.ppermute only.
A program may use at most 256 MiB of HBM per device.

v0:
```python
import math

import jax
import jax.numpy as jnp
from jax import lax
from jax.sharding import PartitionSpec as P

ROT = 32


EPSILON = 1e-05
MASKED = -1e30
ROPE_BASE = 10000.0
CONTRACT_LAST = (((1,), (1,)), ((), ()))
CONTRACT_FIRST = (((0,), (0,)), ((), ()))


def positions(doc_ids):
    length = doc_ids.shape[0]
    places = jnp.arange(length, dtype=jnp.int32)
    change = jnp.concatenate([jnp.ones((1,), dtype=jnp.bool_), doc_ids[1:] != doc_ids[:-1]])
    starts = lax.cummax(jnp.where(change, places, 0), axis=0)
    return places - starts


def rotary_tables(places):
    exponent = jnp.arange(0, ROT, 2, dtype=jnp.float32) / ROT
    inverse = 1.0 / ROPE_BASE**exponent
    angles = places.astype(jnp.float32)[:, None] * inverse[None, :]
    angles = jnp.concatenate([angles, angles], axis=1)
    return (jnp.cos(angles), jnp.sin(angles))


def rotate(field, cos_table, sin_table):
    half_rot = ROT // 2
    turned_part = field[..., :ROT]
    turned = jnp.concatenate([-turned_part[..., half_rot:], turned_part[..., :half_rot]], axis=-1)
    return jnp.concatenate(
        [turned_part * cos_table + turned * sin_table, field[..., ROT:]], axis=-1
    )


def rotate_back(field, cos_table, sin_table):
    half_rot = ROT // 2
    turned_part = field[..., :ROT]
    direct = turned_part * cos_table
    crossed = turned_part * sin_table
    swapped = jnp.concatenate([crossed[..., half_rot:], -crossed[..., :half_rot]], axis=-1)
    return jnp.concatenate([direct + swapped, field[..., ROT:]], axis=-1)


def gelu_slope(pre_act):
    normal_cdf = 0.5 * (1.0 + jax.scipy.special.erf(pre_act * (1.0 / math.sqrt(2.0))))
    return normal_cdf + pre_act * jnp.exp(-0.5 * pre_act * pre_act) * (
        1.0 / math.sqrt(2.0 * math.pi)
    )


def allowed_block(doc_ids, first_row, block_rows):
    key_places = jnp.arange(doc_ids.shape[0], dtype=jnp.int32)
    query_places = first_row + jnp.arange(block_rows, dtype=jnp.int32)
    query_docs = doc_ids[first_row : first_row + block_rows]
    return (key_places[None, :] <= query_places[:, None]) & (
        doc_ids[None, :] == query_docs[:, None]
    )


def masked_scores(query_block, keys_low, allowed, score_scale):
    scores = (
        jnp.einsum("qhd,khd->hqk", query_block, keys_low, preferred_element_type=jnp.float32)
        * score_scale
    )
    return jnp.where(allowed[None], scores, MASKED)


def per_device(
    tokens,
    doc_ids,
    norm1_gain,
    norm1_bias,
    norm2_gain,
    norm2_bias,
    w_qkv,
    b_qkv,
    w_out,
    b_out,
    w_up,
    b_up,
    w_down,
    b_down,
    cotangent,
):
    seq_rows, width_dev = tokens.shape
    model_width = width_dev * lax.axis_size("col")
    rows_weight = w_qkv.shape[0]
    heads_dev = w_qkv.shape[1]
    triple = w_qkv.shape[2]
    head_dim = triple // 3
    ff_dev = w_up.shape[1]
    joint_dev = heads_dev * triple
    attn_dev = heads_dev * head_dim
    block_rows = min(512, seq_rows)
    block_count = seq_rows // block_rows
    score_scale = 1.0 / math.sqrt(head_dim)
    col_offset = lax.axis_index("col") * width_dev
    wq_full, wu_full, wo_full, wd_full, bo_full, bd_full = (
        lax.all_gather(w_qkv.reshape(rows_weight, joint_dev), "row", axis=0, tiled=True),
        lax.all_gather(w_up, "row", axis=0, tiled=True),
        lax.all_gather(w_out, "row", axis=1, tiled=True),
        lax.all_gather(w_down, "row", axis=1, tiled=True),
        lax.all_gather(b_out.reshape(1, -1), "row", axis=1, tiled=True),
        lax.all_gather(b_down.reshape(1, -1), "row", axis=1, tiled=True),
    )
    bias_total = bo_full[0].astype(jnp.float32) + bd_full[0].astype(jnp.float32)
    out_bias = lax.dynamic_slice_in_dim(bias_total, col_offset, width_dev)
    tokens_wide = tokens.astype(jnp.float32)
    row_mean = lax.psum(jnp.sum(tokens_wide, 1), "col") / model_width
    centered = tokens_wide - row_mean[:, None]
    row_var = lax.psum(jnp.sum(centered * centered, 1), "col") / model_width
    inv_std = lax.rsqrt(row_var + EPSILON)
    normed = centered * inv_std[:, None]
    gain_one = norm1_gain.astype(jnp.float32)
    gain_two = norm2_gain.astype(jnp.float32)
    h_first = (normed * gain_one + norm1_bias.astype(jnp.float32)).astype(jnp.bfloat16)
    h_second = (normed * gain_two + norm2_bias.astype(jnp.float32)).astype(jnp.bfloat16)
    joint_parts = []
    up_parts = []
    for block_index in range(block_count):
        first_row = block_index * block_rows
        joint_block = jnp.dot(
            lax.all_gather(h_first[first_row : first_row + block_rows], "col", axis=1, tiled=True),
            wq_full,
            preferred_element_type=jnp.float32,
        )
        up_block = jnp.dot(
            lax.all_gather(h_second[first_row : first_row + block_rows], "col", axis=1, tiled=True),
            wu_full,
            preferred_element_type=jnp.float32,
        )
        joint_parts.append(joint_block)
        up_parts.append(up_block)
    qkv_joint = (
        jnp.concatenate(joint_parts, 0).reshape(seq_rows, heads_dev, triple)
        + b_qkv.astype(jnp.float32)[None]
    )
    pre_act = jnp.concatenate(up_parts, 0) + b_up.astype(jnp.float32)[None]
    gelu_low = jax.nn.gelu(pre_act, approximate=False).astype(jnp.bfloat16)
    cos_table, sin_table = rotary_tables(positions(doc_ids))
    cos_wide = cos_table[:, None, :]
    sin_wide = sin_table[:, None, :]
    queries = rotate(qkv_joint[..., :head_dim], cos_wide, sin_wide).astype(jnp.bfloat16)
    keys_low = rotate(qkv_joint[..., head_dim : 2 * head_dim], cos_wide, sin_wide).astype(
        jnp.bfloat16
    )
    values = qkv_joint[..., 2 * head_dim :].astype(jnp.bfloat16)
    attn_parts = []
    total_parts = []
    for block_index in range(block_count):
        first_row = block_index * block_rows
        allowed = allowed_block(doc_ids, first_row, block_rows)
        scores = masked_scores(
            queries[first_row : first_row + block_rows], keys_low, allowed, score_scale
        )
        row_peak = jnp.max(scores, axis=-1, keepdims=True)
        log_total = row_peak + jnp.log(jnp.sum(jnp.exp(scores - row_peak), axis=-1, keepdims=True))
        probs_low = jnp.exp(scores - log_total).astype(jnp.bfloat16)
        attended = jnp.einsum("hqk,khd->qhd", probs_low, values, preferred_element_type=jnp.float32)
        attn_parts.append(attended.astype(jnp.bfloat16).reshape(block_rows, attn_dev))
        total_parts.append(log_total)
    attn_low = jnp.concatenate(attn_parts, 0)
    out_parts = []
    for block_index in range(block_count):
        first_row = block_index * block_rows
        attn_term = jnp.dot(
            attn_low[first_row : first_row + block_rows],
            wo_full,
            preferred_element_type=jnp.float32,
        )
        mlp_term = jnp.dot(
            gelu_low[first_row : first_row + block_rows],
            wd_full,
            preferred_element_type=jnp.float32,
        )
        attn_share, mlp_share = (
            lax.psum_scatter(attn_term, "col", scatter_dimension=1, tiled=True),
            lax.psum_scatter(mlp_term, "col", scatter_dimension=1, tiled=True),
        )
        branch_total = attn_share + mlp_share
        out_parts.append(
            (
                tokens_wide[first_row : first_row + block_rows] + out_bias[None] + branch_total
            ).astype(jnp.bfloat16)
        )
    layer_out = jnp.concatenate(out_parts, 0)
    acc_wo = jnp.zeros((attn_dev, model_width), jnp.float32)
    acc_wd = jnp.zeros((ff_dev, model_width), jnp.float32)
    acc_bias = jnp.zeros((1, model_width), jnp.float32)
    d_attn_parts = []
    d_pre_parts = []
    for block_index in range(block_count):
        first_row = block_index * block_rows
        attn_block = attn_low[first_row : first_row + block_rows]
        gelu_block = gelu_low[first_row : first_row + block_rows]
        panel_piece = lax.all_gather(
            cotangent[first_row : first_row + block_rows], "col", axis=1, tiled=True
        )
        sum_wo = acc_wo
        sum_wd = acc_wd
        sum_bias = acc_bias
        d_attn = lax.dot_general(
            panel_piece, wo_full, CONTRACT_LAST, preferred_element_type=jnp.float32
        )
        d_gelu = lax.dot_general(
            panel_piece, wd_full, CONTRACT_LAST, preferred_element_type=jnp.float32
        )
        wo_slab = sum_wo + lax.dot_general(
            attn_block, panel_piece, CONTRACT_FIRST, preferred_element_type=jnp.float32
        )
        wd_slab = sum_wd + lax.dot_general(
            gelu_block, panel_piece, CONTRACT_FIRST, preferred_element_type=jnp.float32
        )
        bias_slab = sum_bias + jnp.sum(panel_piece, 0, keepdims=True, dtype=jnp.float32)
        d_attn, d_gelu, acc_wo, acc_wd, acc_bias = (d_attn, d_gelu, wo_slab, wd_slab, bias_slab)
        d_attn_parts.append(d_attn.astype(jnp.bfloat16).reshape(block_rows, heads_dev, head_dim))
        d_pre_parts.append(
            (d_gelu * gelu_slope(pre_act[first_row : first_row + block_rows])).astype(jnp.bfloat16)
        )
    grad_w_out, grad_w_down, bias_grad = (
        lax.psum_scatter(acc_wo, "row", scatter_dimension=1, tiled=True),
        lax.psum_scatter(acc_wd, "row", scatter_dimension=1, tiled=True),
        lax.psum_scatter(acc_bias, "row", scatter_dimension=1, tiled=True),
    )
    d_attn_all = jnp.concatenate(d_attn_parts, 0)
    d_pre = jnp.concatenate(d_pre_parts, 0)
    grad_keys = jnp.zeros((seq_rows, heads_dev, head_dim), jnp.float32)
    grad_values = jnp.zeros((seq_rows, heads_dev, head_dim), jnp.float32)
    grad_query_parts = []
    for block_index in range(block_count):
        first_row = block_index * block_rows
        query_block = queries[first_row : first_row + block_rows]
        d_block = d_attn_all[first_row : first_row + block_rows]
        allowed = allowed_block(doc_ids, first_row, block_rows)
        scores = masked_scores(query_block, keys_low, allowed, score_scale)
        probs_full = jnp.exp(scores - total_parts[block_index])
        probs_low = probs_full.astype(jnp.bfloat16)
        d_probs = jnp.einsum("qhd,khd->hqk", d_block, values, preferred_element_type=jnp.float32)
        row_delta = jnp.sum(probs_full * d_probs, axis=-1, keepdims=True)
        d_scores = (probs_full * (d_probs - row_delta)).astype(jnp.bfloat16)
        grad_query_parts.append(
            jnp.einsum("hqk,khd->qhd", d_scores, keys_low, preferred_element_type=jnp.float32)
            * score_scale
        )
        grad_keys = (
            grad_keys
            + jnp.einsum("hqk,qhd->khd", d_scores, query_block, preferred_element_type=jnp.float32)
            * score_scale
        )
        grad_values = grad_values + jnp.einsum(
            "hqk,qhd->khd", probs_low, d_block, preferred_element_type=jnp.float32
        )
    grad_query = jnp.concatenate(grad_query_parts, 0)
    d_joint = jnp.concatenate(
        [
            rotate_back(grad_query, cos_wide, sin_wide),
            rotate_back(grad_keys, cos_wide, sin_wide),
            grad_values,
        ],
        axis=-1,
    ).astype(jnp.bfloat16)
    d_joint_flat = d_joint.reshape(seq_rows, joint_dev)
    acc_wq = jnp.zeros((model_width, joint_dev), jnp.float32)
    acc_wu = jnp.zeros((model_width, ff_dev), jnp.float32)
    d_norm_one_parts = []
    d_norm_two_parts = []
    for block_index in range(block_count):
        first_row = block_index * block_rows
        dq_block = d_joint_flat[first_row : first_row + block_rows]
        du_block = d_pre[first_row : first_row + block_rows]
        part_one = lax.dot_general(
            dq_block, wq_full, CONTRACT_LAST, preferred_element_type=jnp.float32
        )
        part_two = lax.dot_general(
            du_block, wu_full, CONTRACT_LAST, preferred_element_type=jnp.float32
        )
        wq_slab = acc_wq + lax.dot_general(
            lax.all_gather(h_first[first_row : first_row + block_rows], "col", axis=1, tiled=True),
            dq_block,
            CONTRACT_FIRST,
            preferred_element_type=jnp.float32,
        )
        wu_slab = acc_wu + lax.dot_general(
            lax.all_gather(h_second[first_row : first_row + block_rows], "col", axis=1, tiled=True),
            du_block,
            CONTRACT_FIRST,
            preferred_element_type=jnp.float32,
        )
        acc_wq = wq_slab
        acc_wu = wu_slab
        d_norm_one, d_norm_two = (
            lax.psum_scatter(part_one, "col", scatter_dimension=1, tiled=True),
            lax.psum_scatter(part_two, "col", scatter_dimension=1, tiled=True),
        )
        d_norm_one_parts.append(d_norm_one)
        d_norm_two_parts.append(d_norm_two)
    grad_w_qkv, grad_w_up = (
        lax.psum_scatter(acc_wq, "row", scatter_dimension=0, tiled=True),
        lax.psum_scatter(acc_wu, "row", scatter_dimension=0, tiled=True),
    )
    d_norm_one = jnp.concatenate(d_norm_one_parts, 0)
    d_norm_two = jnp.concatenate(d_norm_two_parts, 0)
    scaled_one = d_norm_one * gain_one
    scaled_two = d_norm_two * gain_two
    sum_one, inner_one, sum_two, inner_two = (
        lax.psum(jnp.sum(scaled_one, 1).astype(jnp.bfloat16), "col").astype(jnp.float32),
        lax.psum(jnp.sum(scaled_one * normed, 1).astype(jnp.bfloat16), "col").astype(jnp.float32),
        lax.psum(jnp.sum(scaled_two, 1).astype(jnp.bfloat16), "col").astype(jnp.float32),
        lax.psum(jnp.sum(scaled_two * normed, 1).astype(jnp.bfloat16), "col").astype(jnp.float32),
    )
    back_one = (
        scaled_one - sum_one[:, None] / model_width - normed * (inner_one[:, None] / model_width)
    )
    back_two = (
        scaled_two - sum_two[:, None] / model_width - normed * (inner_two[:, None] / model_width)
    )
    grad_tokens = (
        cotangent.astype(jnp.float32) + inv_std[:, None] * back_one + inv_std[:, None] * back_two
    )
    local_small = (
        jnp.sum(d_norm_one * normed, 0),
        jnp.sum(d_norm_one, 0),
        jnp.sum(d_norm_two * normed, 0),
        jnp.sum(d_norm_two, 0),
    )
    grad_gain_one, grad_shift_one, grad_gain_two, grad_shift_two, grad_b_qkv, grad_b_up = lax.psum(
        (
            local_small[0],
            local_small[1],
            local_small[2],
            local_small[3],
            jnp.sum(d_joint, 0, dtype=jnp.float32),
            jnp.sum(d_pre, 0, dtype=jnp.float32),
        ),
        "row",
    )
    return (
        layer_out,
        grad_tokens,
        grad_gain_one,
        grad_shift_one,
        grad_gain_two,
        grad_shift_two,
        grad_w_qkv.reshape(rows_weight, heads_dev, triple),
        grad_b_qkv,
        grad_w_out,
        bias_grad[0],
        grad_w_up,
        grad_b_up,
        grad_w_down,
        bias_grad[0],
    )


def solution(mesh):
    placed = (
        P("row", "col"),
        P("row"),
        P("col"),
        P("col"),
        P("col"),
        P("col"),
        P("row", "col", None),
        P("col", None),
        P("col", "row"),
        P("row"),
        P("row", "col"),
        P("col"),
        P("col", "row"),
        P("row"),
        P("row", "col"),
    )
    return jax.shard_map(
        per_device,
        mesh=mesh,
        in_specs=placed,
        out_specs=(
            P("row", "col"),
            P("row", "col"),
            P("col"),
            P("col"),
            P("col"),
            P("col"),
            P("row", "col", None),
            P("col", None),
            P("col", "row"),
            P("row"),
            P("row", "col"),
            P("col"),
            P("col", "row"),
            P("row"),
        ),
        check_vma=False,
    )
```

profile of v0, /device:TPU:0, one launch (start us, length us, event | category | flops | bytes accessed | tf_op | source)
XLA Modules:
  0.0 1777.3 jit_solution(17773284306687932793)
XLA Ops:
  16.4 15.6 psum.84
  32.7 12.4 psum.85
  57.9 5.1 fusion.18
  64.9 6.2 all-gather.49.cloned.1.call-done
  73.1 28.2 %all-gather.47.cloned.1.call-done = bf16[512,2048]{1,0:T(8,128)(2,1)} async-done(((bf16[512,256]{1,0:T(8,128)(2,1)}), bf16[512,2048]{1,0:T(8,128)(2,1)}) %all-gather.47.cloned.1.call-update) | async-done | bytes 2097168 | tf_op jit(solution)/shard_map/all_gather | solution.py:204
  103.2 28.0 %all-gather.45.cloned.1.call-done = bf16[512,2048]{1,0:T(8,128)(2,1)} async-done(((bf16[512,256]{1,0:T(8,128)(2,1)}), bf16[512,2048]{1,0:T(8,128)(2,1)}) %all-gather.45.cloned.1.call-update) | async-done | bytes 2097168 | tf_op jit(solution)/shard_map/all_gather | solution.py:204
  134.8 25.8 %all-gather.31.cloned.1.call-done = bf16[256,2048]{1,0:T(8,128)(2,1)} async-done(((bf16[256,512]{1,0:T(8,128)(2,1)}), bf16[256,2048]{1,0:T(8,128)(2,1)}) %all-gather.31.cloned.1.call-update) | async-done | bytes 1048592 | tf_op jit(solution)/shard_map/all_gather | solution.py:109
  168.6 22.0 %all-gather.21.cloned.1.call-done = bf16[512,2048]{1,0:T(8,128)(2,1)} async-done(((bf16[512,256]{1,0:T(8,128)(2,1)}), bf16[512,2048]{1,0:T(8,128)(2,1)}) %all-gather.21.cloned.1.call-update) | async-done | bytes 2097168 | tf_op jit(solution)/shard_map/all_gather | solution.py:131
  190.6 65.7 %all-gather.23.cloned.1.call-done = bf16[2048,768]{1,0:T(8,128)(2,1)} async-done(((bf16[512,768]{1,0:T(8,128)(2,1)}), bf16[2048,768]{1,0:T(8,128)(2,1)}) %all-gather.23.cloned.1.call-update) | async-done | bytes 3145744 | tf_op jit(solution)/shard_map/all_gather | solution.py:107
  260.6 25.0 %all-gather.25.cloned.1.call-done = bf16[512,2048]{1,0:T(8,128)(2,1)} async-done(((bf16[512,256]{1,0:T(8,128)(2,1)}), bf16[512,2048]{1,0:T(8,128)(2,1)}) %all-gather.25.cloned.1.call-update) | async-done | bytes 2097168 | tf_op jit(solution)/shard_map/all_gather | solution.py:131
  285.6 5.4 fusion.139
  291.1 24.7 %all-gather.27.cloned.1.call-done = bf16[512,2048]{1,0:T(8,128)(2,1)} async-done(((bf16[512,256]{1,0:T(8,128)(2,1)}), bf16[512,2048]{1,0:T(8,128)(2,1)}) %all-gather.27.cloned.1.call-update) | async-done | bytes 2097168 | tf_op jit(solution)/shard_map/all_gather | solution.py:131
  315.7 5.4 fusion.140
  321.2 25.1 %all-gather.29.cloned.1.call-done = bf16[512,2048]{1,0:T(8,128)(2,1)} async-done(((bf16[512,256]{1,0:T(8,128)(2,1)}), bf16[512,2048]{1,0:T(8,128)(2,1)}) %all-gather.29.cloned.1.call-update) | async-done | bytes 2097168 | tf_op jit(solution)/shard_map/all_gather | solution.py:131
  372.0 5.8 multiply_reduce_fusion.3
  383.8 5.8 multiply_reduce_fusion.2
  389.6 17.4 multiply_convert_fusion.2
  429.1 6.7 multiply_reduce_fusion.1
  435.8 5.8 multiply_reduce_fusion
  441.6 17.6 multiply_convert_fusion
  500.2 7.7 fusion.26
  516.2 6.0 fusion.147
  522.5 6.1 fusion.148
  529.2 6.0 fusion.149
  535.3 6.7 fusion.142
  542.0 6.5 fusion.143
  548.6 6.5 fusion.144
  555.1 5.8 fusion.145
  560.9 20.1 %fusion.2 = (bf16[2048,1024]{1,0:T(8,128)(2,1)}, f32[2048,1024]{1,0:T(8,128)}) fusion(f32[1024]{0:T(1024)S(1)} %convert_element_type.196, f32[512,1024]{1,0:T(8,128)S(1)} %fusion.145, f32[512,1024]{1,0:T(8,128)S(1)} %copy-done.53, f32[512,1024]{1,0:T(8,128)S(1)} %copy-done.52, f32[512,1024]{1,0:T(8,128)S(1)} %copy-done.51), kind=kLoop, calls=%fused_computation.3 | loop fusion | flops 144703488 | bytes 20975616 | tf_op jit(solution)/shard_map/convert_element_type | solution.py:147
  580.9 48.4 %all-gather.43.cloned.1.call-done = bf16[1024,2048]{1,0:T(8,128)(2,1)} async-done(((bf16[1024,512]{1,0:T(8,128)(2,1)}), bf16[1024,2048]{1,0:T(8,128)(2,1)}) %all-gather.43.cloned.1.call-update) | async-done | bytes 4194320 | tf_op jit(solution)/shard_map/all_gather | solution.py:110
  629.4 6.4 fusion.32
  641.2 6.5 fusion.38
  648.7 4.5 fusion.151
  653.4 6.5 fusion.44
  665.4 7.3 fusion.50
  678.4 6.8 convolution_convert_fusion.5
  691.7 6.6 convolution_convert_fusion.4
  705.3 6.6 convolution_convert_fusion.6
  719.5 7.2 convolution_convert_fusion.7
  741.8 4.9 add_add_fusion.2
  760.2 5.7 fusion.159
  766.0 5.7 fusion.160
  771.7 13.4 add_add_fusion.1
  785.5 4.5 fusion.64
  790.0 5.7 fusion.68
  795.7 5.7 fusion.72
  801.4 12.7 add_add_fusion
  816.9 11.9 all-gather.2
  828.8 12.2 all-gather.3
  850.0 25.1 %reduce-scatter.26.cloned.1.call-done = f32[512,256]{1,0:T(8,128)} async-done(((f32[512,2048]{1,0:T(8,128)}), f32[512,256]{1,0:T(8,128)}) %reduce-scatter.26.cloned.1.call-update) | async-done | bytes 524304 | tf_op jit(solution)/shard_map/reduce_scatter | solution.py:300
  876.3 54.0 %reduce-scatter.28.cloned.1.call-done = f32[512,256]{1,0:T(8,128)} async-done(((f32[512,2048]{1,0:T(8,128)}), f32[512,256]{1,0:T(8,128)}) %reduce-scatter.28.cloned.1.call-update) | async-done | bytes 524304 | tf_op jit(solution)/shard_map/reduce_scatter | solution.py:301
  932.1 52.8 %reduce-scatter.30.cloned.1.call-done = f32[512,256]{1,0:T(8,128)} async-done(((f32[512,2048]{1,0:T(8,128)}), f32[512,256]{1,0:T(8,128)}) %reduce-scatter.30.cloned.1.call-update) | async-done | bytes 524304 | tf_op jit(solution)/shard_map/reduce_scatter | solution.py:301
  986.8 53.1 %reduce-scatter.32.cloned.1.call-done = f32[512,256]{1,0:T(8,128)} async-done(((f32[512,2048]{1,0:T(8,128)}), f32[512,256]{1,0:T(8,128)}) %reduce-scatter.32.cloned.1.call-update) | async-done | bytes 524304 | tf_op jit(solution)/shard_map/reduce_scatter | solution.py:301
  1041.8 52.8 %reduce-scatter.34.cloned.1.call-done = f32[512,256]{1,0:T(8,128)} async-done(((f32[512,2048]{1,0:T(8,128)}), f32[512,256]{1,0:T(8,128)}) %reduce-scatter.34.cloned.1.call-update) | async-done | bytes 524304 | tf_op jit(solution)/shard_map/reduce_scatter | solution.py:301
  1099.8 19.3 %all-reduce = (f32[256]{0:T(256)}, f32[256]{0:T(256)}, f32[256]{0:T(256)}, f32[256]{0:T(256)}, f32[2,384]{1,0:T(2,128)}, /*index=5*/f32[1024]{0:T(1024)}) all-reduce(f32[256]{0:T(256)S(1)} %get-tuple-element.22, f32[256]{0:T(256)S(1)} %add_add_fusion.5, f32[256]{0:T(256)S(1)} %get-tuple-element.14, ...), channel_id=1, replica_groups=mesh['row'=4,'col'=8] {'row'}, use_global_device_ids=true, to_apply=%region_43.44 | all-reduce | flops 2816 | bytes 22528 | tf_op jit(solution)/shard_map/psum | solution.py:334
  1119.1 22.8 %all-reduce.1 = (bf16[2048]{0:T(1024)(128)(2,1)S(1)}, bf16[2048]{0:T(1024)(128)(2,1)S(1)}, bf16[2048]{0:T(1024)(128)(2,1)S(1)}, bf16[2048]{0:T(1024)(128)(2,1)S(1)}) all-reduce(bf16[2048]{0:T(1024)(128)(2,1)S(1)} %get-tuple-element.15, bf16[2048]{0:T(1024)(128)(2,1)S(1)} %get-tuple-element.19, ...), channel_id=1, replica_groups=mesh['row'=4,'col'=8] {'col'}, use_global_device_ids=true, to_apply=%region_41.42 | all-reduce | flops 8192 | bytes 32768 | tf_op jit(solution)/shard_map/psum | solution.py:317
  1142.0 7.9 reduce-scatter.48.cloned.1.call-done
  1149.9 54.5 %reduce-scatter.50.cloned.1.call-done = f32[512,256]{1,0:T(8,128)} async-done(((f32[512,2048]{1,0:T(8,128)}), f32[512,256]{1,0:T(8,128)}) %reduce-scatter.50.cloned.1.call-update) | async-done | bytes 524304 | tf_op jit(solution)/shard_map/reduce_scatter | solution.py:185
  1204.4 55.1 %reduce-scatter.46.cloned.1.call-done = f32[512,256]{1,0:T(8,128)} async-done(((f32[512,2048]{1,0:T(8,128)}), f32[512,256]{1,0:T(8,128)}) %reduce-scatter.46.cloned.1.call-update) | async-done | bytes 524304 | tf_op jit(solution)/shard_map/reduce_scatter | solution.py:185
  1259.5 54.7 %reduce-scatter.44.cloned.1.call-done = f32[512,256]{1,0:T(8,128)} async-done(((f32[512,2048]{1,0:T(8,128)}), f32[512,256]{1,0:T(8,128)}) %reduce-scatter.44.cloned.1.call-update) | async-done | bytes 524304 | tf_op jit(solution)/shard_map/reduce_scatter | solution.py:185
  1321.0 106.2 %reduce-scatter.36.cloned.1.call-done = f32[512,768]{1,0:T(8,128)} async-done(((f32[2048,768]{1,0:T(8,128)}), f32[512,768]{1,0:T(8,128)}) %reduce-scatter.36.cloned.1.call-update) | async-done | bytes 1572880 | tf_op jit(solution)/shard_map/reduce_scatter | solution.py:306
  1430.1 44.5 %reduce-scatter.38.cloned.1.call-done = f32[256,512]{1,0:T(8,128)} async-done(((f32[256,2048]{1,0:T(8,128)}), f32[256,512]{1,0:T(8,128)}) %reduce-scatter.38.cloned.1.call-update) | async-done | bytes 524304 | tf_op jit(solution)/shard_map/reduce_scatter | solution.py:229
  1474.6 146.8 %reduce-scatter.40.cloned.1.call-done = f32[512,1024]{1,0:T(8,128)} async-done(((f32[2048,1024]{1,0:T(8,128)}), f32[512,1024]{1,0:T(8,128)}) %reduce-scatter.40.cloned.1.call-update) | async-done | bytes 2097168 | tf_op jit(solution)/shard_map/reduce_scatter | solution.py:307
  1621.4 148.0 %reduce-scatter.42.cloned.1.call-done = f32[1024,512]{1,0:T(8,128)} async-done(((f32[1024,2048]{1,0:T(8,128)}), f32[1024,512]{1,0:T(8,128)}) %reduce-scatter.42.cloned.1.call-update) | async-done | bytes 2097168 | tf_op jit(solution)/shard_map/reduce_scatter | solution.py:230
  (429 shorter events, 249.2 us)
Async XLA Ops:
  7.2 24.9 %copy-start.15 = (bf16[2048,256]{1,0:T(8,128)(2,1)S(1)}, bf16[2048,256]{1,0:T(8,128)(2,1)}, u32[]{:S(2)}) copy-start(bf16[2048,256]{1,0:T(8,128)(2,1)} %param.15) | copy-start | bytes 3145732
  7.2 55.8 %all-gather.51.cloned.1.call-start = ((), (), s32[]{:S(2)}) async-start(), calls=%async_computation.32 | async-start | bytes 2359296 | tf_op jit(solution)/shard_map/all_gather | solution.py:204
  9.5 61.6 %all-gather.49.cloned.1.call-start = ((), (), s32[]{:S(2)}) async-start(), calls=%async_computation.31 | async-start | bytes 2359296 | tf_op jit(solution)/shard_map/all_gather | solution.py:204
  10.3 91.0 %all-gather.47.cloned.1.call-start = ((), (), s32[]{:S(2)}) async-start(), calls=%async_computation.30 | async-start | bytes 2359296 | tf_op jit(solution)/shard_map/all_gather | solution.py:204
  11.0 35.9 %copy-start.69 = (bf16[512,2,384]{2,1,0:T(2,128)(2,1)S(1)}, bf16[512,2,384]{2,1,0:T(2,128)(2,1)}, u32[]{:S(2)}) copy-start(bf16[512,2,384]{2,1,0:T(2,128)(2,1)} %param.21) | copy-start | bytes 2359300
  11.0 120.2 %all-gather.45.cloned.1.call-start = ((), (), s32[]{:S(2)}) async-start(), calls=%async_computation.29 | async-start | bytes 2359296 | tf_op jit(solution)/shard_map/all_gather | solution.py:204
  11.6 149.0 %all-gather.31.cloned.1.call-start = ((), (), s32[]{:S(2)}) async-start(), calls=%async_computation.22 | async-start | bytes 1310720 | tf_op jit(solution)/shard_map/all_gather | solution.py:109
  12.2 178.4 %all-gather.21.cloned.1.call-start = ((), (), s32[]{:S(2)}) async-start(), calls=%async_computation.17 | async-start | bytes 2359296 | tf_op jit(solution)/shard_map/all_gather | solution.py:131
  12.9 35.1 %copy-start.82 = (f32[256]{0:T(256)}, f32[256]{0:T(256)S(1)}, u32[]{:S(2)}) copy-start(f32[256]{0:T(256)S(1)} %convert_element_type.185) | copy-start | bytes 3076
  13.5 34.4 %copy-start.84 = (f32[256]{0:T(256)}, f32[256]{0:T(256)S(1)}, u32[]{:S(2)}) copy-start(f32[256]{0:T(256)S(1)} %convert_element_type.193) | copy-start | bytes 3076
  32.0 16.0 copy-start.75
  46.9 209.4 %all-gather.23.cloned.1.call-start = ((), (), s32[]{:S(2)}) async-start(), calls=%async_computation.18 | async-start | bytes 3932160 | tf_op jit(solution)/shard_map/all_gather | solution.py:107
  46.9 7.3 copy-start.88
  47.0 7.3 copy-start.79
  48.0 237.6 %all-gather.25.cloned.1.call-start = ((), (), s32[]{:S(2)}) async-start(), calls=%async_computation.19 | async-start | bytes 2359296 | tf_op jit(solution)/shard_map/all_gather | solution.py:131
  48.8 267.0 %all-gather.27.cloned.1.call-start = ((), (), s32[]{:S(2)}) async-start(), calls=%async_computation.20 | async-start | bytes 2359296 | tf_op jit(solution)/shard_map/all_gather | solution.py:131
  49.5 296.8 %all-gather.29.cloned.1.call-start = ((), (), s32[]{:S(2)}) async-start(), calls=%async_computation.21 | async-start | bytes 2359296 | tf_op jit(solution)/shard_map/all_gather | solution.py:131
  50.1 485.2 %all-gather.33.cloned.1.call-start = ((), (), s32[]{:S(2)}) async-start(), calls=%async_computation.23 | async-start | bytes 2359296 | tf_op jit(solution)/shard_map/all_gather | solution.py:136
  51.1 484.2 %all-gather.35.cloned.1.call-start = ((), (), s32[]{:S(2)}) async-start(), calls=%async_computation.24 | async-start | bytes 5242880 | tf_op jit(solution)/shard_map/all_gather | solution.py:108
  51.7 490.3 %all-gather.37.cloned.1.call-start = ((), (), s32[]{:S(2)}) async-start(), calls=%async_computation.25 | async-start | bytes 2359296 | tf_op jit(solution)/shard_map/all_gather | solution.py:136
  52.5 496.1 %all-gather.39.cloned.1.call-start = ((), (), s32[]{:S(2)}) async-start(), calls=%async_computation.26 | async-start | bytes 2359296 | tf_op jit(solution)/shard_map/all_gather | solution.py:136
  53.0 502.0 %all-gather.41.cloned.1.call-start = ((), (), s32[]{:S(2)}) async-start(), calls=%async_computation.27 | async-start | bytes 2359296 | tf_op jit(solution)/shard_map/all_gather | solution.py:136
  53.6 575.7 %all-gather.43.cloned.1.call-start = ((), (), s32[]{:S(2)}) async-start(), calls=%async_computation.28 | async-start | bytes 5242880 | tf_op jit(solution)/shard_map/all_gather | solution.py:110
  54.2 786.8 %reduce-scatter.52.cloned.1.call-start = ((), (), s32[]{:S(2)}) async-start(), calls=%async_computation.49 | async-start | bytes 1310720
  57.8 299.5 %copy-start.27 = (f32[2048,32]{1,0:T(8,128)}, f32[2048,32]{1,0:T(8,128)S(1)}, u32[]{:S(2)}) copy-start(f32[2048,32]{1,0:T(8,128)S(1)} %copy.132) | copy-start | bytes 786436
  133.2 30.8 %copy-start.33 = (bf16[512,2048]{1,0:T(8,128)(2,1)S(1)}, bf16[512,2048]{1,0:T(8,128)(2,1)}, u32[]{:S(2)}) copy-start(bf16[512,2048]{1,0:T(8,128)(2,1)} %all-gather.47.cloned.1.call-done) | copy-start | bytes 6291460
  134.5 711.9 %reduce-scatter.20.cloned.1.call-start = ((), (), s32[]{:S(2)}) async-start(), calls=%async_computation.33 | async-start | bytes 4718592 | tf_op jit(solution)/shard_map/reduce_scatter | solution.py:300
  352.3 30.7 %copy-start.17 = (bf16[2048,2,384]{2,0,1:T(8,128)(2,1)}, bf16[2048,2,384]{2,0,1:T(8,128)(2,1)S(1)}, u32[]{:S(2)}) copy-start(bf16[2048,2,384]{2,0,1:T(8,128)(2,1)S(1)} %get-tuple-element.33) | copy-start | bytes 9437188
  365.3 6.7 copy-start
  367.9 21.6 %copy-start.80 = (f32[2,512]{1,0:T(2,128)}, f32[2,512]{1,0:T(2,128)S(1)}, u32[]{:S(2)}) copy-start(f32[2,512]{1,0:T(2,128)S(1)} %log_add_fusion.3) | copy-start | bytes 12292
  417.0 12.2 copy-start.2
  421.8 14.0 copy-start.3
  429.1 6.7 copy-start.20
  429.1 6.7 copy-start.70
  472.9 6.7 slice-start.2
  489.2 11.0 copy-start.21
  516.2 331.5 %reduce-scatter.22.cloned.1.call-start = ((), (), s32[]{:S(2)}) async-start(), calls=%async_computation.34 | async-start | bytes 4718592 | tf_op jit(solution)/shard_map/reduce_scatter | solution.py:300
  522.2 326.6 %reduce-scatter.24.cloned.1.call-start = ((), (), s32[]{:S(2)}) async-start(), calls=%async_computation.35 | async-start | bytes 4718592 | tf_op jit(solution)/shard_map/reduce_scatter | solution.py:300
  528.6 346.5 %reduce-scatter.26.cloned.1.call-start = ((), (), s32[]{:S(2)}) async-start(), calls=%async_computation.36 | async-start | bytes 4718592 | tf_op jit(solution)/shard_map/reduce_scatter | solution.py:300
  535.2 395.0 %reduce-scatter.28.cloned.1.call-start = ((), (), s32[]{:S(2)}) async-start(), calls=%async_computation.37 | async-start | bytes 4718592 | tf_op jit(solution)/shard_map/reduce_scatter | solution.py:301
  629.4 7.4 copy-start.95
  641.2 343.8 %reduce-scatter.30.cloned.1.call-start = ((), (), s32[]{:S(2)}) async-start(), calls=%async_computation.38 | async-start | bytes 4718592 | tf_op jit(solution)/shard_map/reduce_scatter | solution.py:301
  641.2 7.5 copy-start.96
  653.2 386.7 %reduce-scatter.32.cloned.1.call-start = ((), (), s32[]{:S(2)}) async-start(), calls=%async_computation.39 | async-start | bytes 4718592 | tf_op jit(solution)/shard_map/reduce_scatter | solution.py:301
  653.4 7.5 copy-start.97
  665.3 429.2 %reduce-scatter.34.cloned.1.call-start = ((), (), s32[]{:S(2)}) async-start(), calls=%async_computation.40 | async-start | bytes 4718592 | tf_op jit(solution)/shard_map/reduce_scatter | solution.py:301
  665.4 8.3 copy-start.98
  678.1 471.8 %reduce-scatter.48.cloned.1.call-start = ((), (), s32[]{:S(2)}) async-start(), calls=%async_computation.47 | async-start | bytes 4718592 | tf_op jit(solution)/shard_map/reduce_scatter | solution.py:185
  678.4 6.8 copy-start.91
  691.7 512.7 %reduce-scatter.50.cloned.1.call-start = ((), (), s32[]{:S(2)}) async-start(), calls=%async_computation.48 | async-start | bytes 4718592 | tf_op jit(solution)/shard_map/reduce_scatter | solution.py:185
  704.8 554.7 %reduce-scatter.46.cloned.1.call-start = ((), (), s32[]{:S(2)}) async-start(), calls=%async_computation.46 | async-start | bytes 4718592 | tf_op jit(solution)/shard_map/reduce_scatter | solution.py:185
  705.3 6.6 copy-start.93
  718.3 595.9 %reduce-scatter.44.cloned.1.call-start = ((), (), s32[]{:S(2)}) async-start(), calls=%async_computation.45 | async-start | bytes 4718592 | tf_op jit(solution)/shard_map/reduce_scatter | solution.py:185
  719.5 7.2 copy-start.94
  733.2 694.0 %reduce-scatter.36.cloned.1.call-start = ((), (), s32[]{:S(2)}) async-start(), calls=%async_computation.41 | async-start | bytes 7864320 | tf_op jit(solution)/shard_map/reduce_scatter | solution.py:306
  746.7 727.9 %reduce-scatter.38.cloned.1.call-start = ((), (), s32[]{:S(2)}) async-start(), calls=%async_computation.42 | async-start | bytes 2621440 | tf_op jit(solution)/shard_map/reduce_scatter | solution.py:229
  755.5 865.8 %reduce-scatter.40.cloned.1.call-start = ((), (), s32[]{:S(2)}) async-start(), calls=%async_computation.43 | async-start | bytes 10485760 | tf_op jit(solution)/shard_map/reduce_scatter | solution.py:307
  785.2 984.2 %reduce-scatter.42.cloned.1.call-start = ((), (), s32[]{:S(2)}) async-start(), calls=%async_computation.44 | async-start | bytes 10485760 | tf_op jit(solution)/shard_map/reduce_scatter | solution.py:230
  814.2 30.3 %copy-start.60 = (bf16[512,1024]{1,0:T(8,128)(2,1)S(1)}, bf16[512,1024]{1,0:T(8,128)(2,1)}, u32[]{:S(2)}) copy-start(bf16[512,1024]{1,0:T(8,128)(2,1)} %copy-done.58) | copy-start | bytes 3145732
  842.1 927.3 %copy-start.86 = (f32[1,512]{1,0:T(1,128)}, f32[1,512]{1,0:T(1,128)S(1)}, u32[]{:S(2)}) copy-start(f32[1,512]{1,0:T(1,128)S(1)} %copy.186) | copy-start | bytes 6148
  846.4 250.1 %copy-start.76 = (f32[2048]{0:T(1024)S(1)}, f32[2048]{0:T(1024)}, u32[]{:S(2)}) copy-start(f32[2048]{0:T(1024)} %copy-done.75) | copy-start | bytes 24580
  846.4 250.1 %copy-start.78 = (f32[2048]{0:T(1024)S(1)}, f32[2048]{0:T(1024)}, u32[]{:S(2)}) copy-start(f32[2048]{0:T(1024)} %copy-done.77) | copy-start | bytes 24580
  846.4 250.1 %copy-start.83 = (f32[256]{0:T(256)S(1)}, f32[256]{0:T(256)}, u32[]{:S(2)}) copy-start(f32[256]{0:T(256)} %copy-done.82) | copy-start | bytes 3076
  846.4 250.1 %copy-start.85 = (f32[256]{0:T(256)S(1)}, f32[256]{0:T(256)}, u32[]{:S(2)}) copy-start(f32[256]{0:T(256)} %copy-done.84) | copy-start | bytes 3076
  (76 other events, 238.7 us)
Sparse Core Ops, SparseCore 0:
  9.9 31.0 all-gather.50
  42.9 28.1 all-gather.48
  73.0 28.1 all-gather.46
  103.0 28.1 all-gather.44
  132.6 27.9 all-gather.30
  162.9 27.6 all-gather.20
  192.8 63.4 all-gather.22
  258.7 26.8 all-gather.24
  287.5 28.1 all-gather.26
  318.0 28.1 all-gather.28
  348.2 28.1 all-gather.32
  377.8 80.7 all-gather.34
  460.5 26.7 all-gather.36
  489.0 28.1 all-gather.38
  518.9 28.1 all-gather.40
  548.6 80.7 all-gather.42
  631.5 25.6 reduce-scatter.51
  660.8 49.9 reduce-scatter.19
  714.2 51.2 reduce-scatter.21
  769.1 51.3 reduce-scatter.23
  823.8 51.2 reduce-scatter.25
  878.8 51.3 reduce-scatter.27
  933.6 51.2 reduce-scatter.29
  988.5 51.3 reduce-scatter.31
  1043.2 51.2 reduce-scatter.33
  1098.2 51.6 reduce-scatter.47
  1153.1 51.2 reduce-scatter.49
  1208.1 51.3 reduce-scatter.45
  1262.9 51.2 reduce-scatter.43
  1316.4 110.7 reduce-scatter.35
  1430.2 44.3 reduce-scatter.37
  1477.5 143.7 reduce-scatter.39
  1624.1 145.1 reduce-scatter.41
where the time goes:
time: 1780 us
  waiting for transfers between devices  1160 us (65%)
  matrix products  320 us (18%)
  other arithmetic  128 us (7%)
  blocking collectives  94.2 us (5%)
  local copies, waits for them, and re-layouts  53.2 us (3%)
    reduce_scatter x4, waiting for transfers between devices, per_device(): lax.psum_scatter(part_two, 'col', scatter_dimension=1, tiled=True)  213 us
    reduce_scatter x4, waiting for transfers between devices, per_device(): lax.psum_scatter(attn_term, 'col', scatter_dimension=1, tiled=True)  172 us
    reduce_scatter x1, waiting for transfers between devices, per_device(): lax.psum_scatter(acc_wd, 'row', scatter_dimension=1, tiled=True)  148 us
    reduce_scatter x1, waiting for transfers between devices, per_device(): lax.psum_scatter(acc_wu, 'row', scatter_dimension=0, tiled=True)  147 us
    reduce_scatter x1, waiting for transfers between devices, per_device(): lax.psum_scatter(acc_wq, 'row', scatter_dimension=0, tiled=True)  106 us
    all_gather x4, waiting for transfers between devices, per_device(): lax.all_gather(h_first[first_row:first_row + block_rows], 'col', axis=1,...  96.8 us
    all_gather x1, waiting for transfers between devices, per_device(): lax.all_gather(w_qkv.reshape(rows_weight, joint_dev), 'row', axis=0, tile...  65.7 us
    all_gather x4, waiting for transfers between devices, per_device(): lax.all_gather(cotangent[first_row:first_row + block_rows], 'col', axis=1...  62.4 us
  transfers between devices with their start and end apart: 33, of which 23 were waited for; matrix products, arithmetic and copies ran while one was open for 27% of the time, Pallas kernels for 0%

commit v1 on v0

v1 whole, which is shorter than its diff:
```python
import functools
import math

import jax
import jax.numpy as jnp
from jax import lax
from jax.experimental import pallas as pl
from jax.experimental.pallas import tpu as pltpu
from jax.sharding import PartitionSpec as P

ROT = 32
EPSILON = 1e-05
MASKED = -1e30
ROPE_BASE = 10000.0
DOC_MAX = 1024
NT = (((1,), (1,)), ((), ()))
TN = (((0,), (0,)), ((), ()))
F32 = jnp.float32
BF16 = jnp.bfloat16
VMEM_LIMIT = 56 * 1024 * 1024


def run_starts(doc_ids):
    places = jnp.arange(doc_ids.shape[0], dtype=jnp.int32)
    change = jnp.concatenate([jnp.ones((1,), dtype=jnp.bool_), doc_ids[1:] != doc_ids[:-1]])
    return lax.cummax(jnp.where(change, places, 0), axis=0)


def rotary_tables(places, head_dim):
    exponent = jnp.arange(0, ROT, 2, dtype=F32) / ROT
    inverse = 1.0 / ROPE_BASE**exponent
    angles = inverse[:, None] * places.astype(F32)[None, :]
    cos, sin = jnp.cos(angles).T, jnp.sin(angles).T
    rest = (places.shape[0], head_dim - ROT)
    return (
        jnp.concatenate([cos, cos, jnp.ones(rest, F32)], axis=1),
        jnp.concatenate([sin, sin, jnp.zeros(rest, F32)], axis=1),
    )


def turn(field, cos, sin):
    half = ROT // 2
    width = field.shape[1]
    lane = lax.broadcasted_iota(jnp.int32, field.shape, 1)
    swapped = jnp.where(
        lane < half, -pltpu.roll(field, width - half, 1), pltpu.roll(field, half, 1)
    )
    return field * cos + swapped * sin


def turn_back(field, cos, sin):
    half = ROT // 2
    width = field.shape[1]
    lane = lax.broadcasted_iota(jnp.int32, field.shape, 1)
    crossed = field * sin
    swapped = jnp.where(
        lane < half,
        pltpu.roll(crossed, width - half, 1),
        jnp.where(lane < ROT, -pltpu.roll(crossed, half, 1), 0.0),
    )
    return field * cos + swapped


def attention_body(
    block,
    most,
    scale,
    low_ref,
    start_ref,
    q_ref,
    k_ref,
    v_ref,
    grad_ref,
    cos_q_ref,
    sin_q_ref,
    cos_k_ref,
    sin_k_ref,
    out_ref,
    joint_ref,
    key_ref,
    key_t_ref,
    val_ref,
    val_t_ref,
    dk_ref,
    dv_ref,
):
    step = pl.program_id(1)
    head_dim = q_ref.shape[1]

    @pl.when(step == 0)
    def _():
        turned = turn(k_ref[...], cos_k_ref[...], sin_k_ref[...])
        key_ref[...] = turned.astype(BF16)
        key_t_ref[...] = turned.T.astype(BF16)
        val_ref[...] = v_ref[...].astype(BF16)
        val_t_ref[...] = v_ref[...].T.astype(BF16)
        dk_ref[...] = jnp.zeros_like(dk_ref)
        dv_ref[...] = jnp.zeros_like(dv_ref)

    cos_q = cos_q_ref[...]
    sin_q = sin_q_ref[...]
    low = low_ref[step]
    count = step - low + 1
    rows = pl.ds(pl.multiple_of(step * block, block), block)

    def attend(blocks):
        query = turn(q_ref[...], cos_q, sin_q).astype(BF16)
        grad = grad_ref[...]
        length = blocks * block
        first = pl.multiple_of(low * block, block)
        span = pl.ds(first, length)
        scores = lax.dot_general(key_ref[span, :], query, NT, preferred_element_type=F32) * scale
        key_place = first + lax.broadcasted_iota(jnp.int32, scores.shape, 0)
        query_place = step * block + lax.broadcasted_iota(jnp.int32, scores.shape, 1)
        allowed = (key_place <= query_place) & (key_place >= start_ref[...])
        scores = jnp.where(allowed, scores, MASKED)
        peak = jnp.max(scores, axis=0, keepdims=True)
        raised = jnp.exp(scores - peak)
        probs = raised * (1.0 / jnp.sum(raised, axis=0, keepdims=True))
        probs_low = probs.astype(BF16)
        attended = jnp.dot(val_t_ref[:, span], probs_low, preferred_element_type=F32)
        out_ref[...] = attended.T.astype(BF16)
        d_probs = lax.dot_general(val_ref[span, :], grad, NT, preferred_element_type=F32)
        delta = jnp.sum(probs * d_probs, axis=0, keepdims=True)
        d_scores = (probs * (d_probs - delta)).astype(BF16)
        d_query = jnp.dot(key_t_ref[:, span], d_scores, preferred_element_type=F32).T * scale
        joint_ref[rows, 0:head_dim] = turn_back(d_query, cos_q, sin_q).astype(BF16)
        dk_ref[span, :] += jnp.dot(d_scores, query, preferred_element_type=F32)
        dv_ref[span, :] += jnp.dot(probs_low, grad, preferred_element_type=F32)

    for blocks in range(1, most + 1):
        pl.when(count == blocks)(functools.partial(attend, blocks))

    @pl.when(step == pl.num_programs(1) - 1)
    def _():
        d_key = turn_back(dk_ref[...] * scale, cos_k_ref[...], sin_k_ref[...])
        joint_ref[:, head_dim : 2 * head_dim] = d_key.astype(BF16)
        joint_ref[:, 2 * head_dim :] = dv_ref[...].astype(BF16)


def attention(qkv, d_attn, starts, cos, sin, head_dim):
    length = qkv.shape[0]
    heads = qkv.shape[1] // (3 * head_dim)
    block = min(256, length)
    steps = length // block
    most = min(steps, DOC_MAX // block + 1)
    low = (starts[::block] // block).astype(jnp.int32)
    whole = lambda part: pl.BlockSpec((length, head_dim), lambda h, i, low: (0, 3 * h + part))
    tile = pl.BlockSpec((block, head_dim), lambda h, i, low: (i, h))
    table = pl.BlockSpec((block, head_dim), lambda h, i, low: (i, 0))
    full_table = pl.BlockSpec((length, head_dim), lambda h, i, low: (0, 0))
    return pl.pallas_call(
        functools.partial(attention_body, block, most, 1.0 / math.sqrt(head_dim)),
        out_shape=(
            jax.ShapeDtypeStruct((length, heads * head_dim), BF16),
            jax.ShapeDtypeStruct((length, heads * 3 * head_dim), BF16),
        ),
        grid_spec=pltpu.PrefetchScalarGridSpec(
            num_scalar_prefetch=1,
            grid=(heads, steps),
            in_specs=[
                pl.BlockSpec((1, block), lambda h, i, low: (0, i)),
                pl.BlockSpec((block, head_dim), lambda h, i, low: (i, 3 * h)),
                whole(1),
                whole(2),
                tile,
                table,
                table,
                full_table,
                full_table,
            ],
            out_specs=(
                tile,
                pl.BlockSpec((length, 3 * head_dim), lambda h, i, low: (0, h)),
            ),
            scratch_shapes=[
                pltpu.VMEM((length, head_dim), BF16),
                pltpu.VMEM((head_dim, length), BF16),
                pltpu.VMEM((length, head_dim), BF16),
                pltpu.VMEM((head_dim, length), BF16),
                pltpu.VMEM((length, head_dim), F32),
                pltpu.VMEM((length, head_dim), F32),
            ],
        ),
        compiler_params=pltpu.CompilerParams(
            dimension_semantics=("arbitrary", "arbitrary"), vmem_limit_bytes=VMEM_LIMIT
        ),
        cost_estimate=pl.CostEstimate(
            flops=heads * length * 3 * block * head_dim * 10,
            bytes_accessed=heads * length * head_dim * 24,
            transcendentals=heads * length * 3 * block,
        ),
        name="attention",
    )(low, starts[None, :], qkv, qkv, qkv, d_attn, cos, sin, cos, sin)


def norm_body(x_ref, affine_ref, one_ref, two_ref, stat_ref):
    x = x_ref[...].astype(F32)
    mean = jnp.mean(x, axis=1, keepdims=True)
    centered = x - mean
    scale = lax.rsqrt(jnp.mean(centered * centered, axis=1, keepdims=True) + EPSILON)
    normed = centered * scale
    affine = affine_ref[...].astype(F32)
    one_ref[...] = (normed * affine[0:1] + affine[1:2]).astype(BF16)
    two_ref[...] = (normed * affine[2:3] + affine[3:4]).astype(BF16)
    stat_ref[...] = jnp.concatenate([mean, scale], axis=1)


def normalize(x, affine):
    length, width = x.shape
    block = min(256, length)
    rows = pl.BlockSpec((block, width), lambda i: (i, 0))
    return pl.pallas_call(
        norm_body,
        out_shape=(
            jax.ShapeDtypeStruct((length, width), BF16),
            jax.ShapeDtypeStruct((length, width), BF16),
            jax.ShapeDtypeStruct((length, 2), F32),
        ),
        grid=(length // block,),
        in_specs=[rows, pl.BlockSpec(affine.shape, lambda i: (0, 0))],
        out_specs=(rows, rows, pl.BlockSpec((block, 2), lambda i: (i, 0))),
        compiler_params=pltpu.CompilerParams(vmem_limit_bytes=VMEM_LIMIT),
        cost_estimate=pl.CostEstimate(
            flops=10 * length * width, bytes_accessed=6 * length * width, transcendentals=length
        ),
        name="normalize",
    )(x, affine)


def gelu_slope(pre_act):
    normal_cdf = 0.5 * (1.0 + lax.erf(pre_act * (1.0 / math.sqrt(2.0))))
    density = jnp.exp(-0.5 * pre_act * pre_act) * (1.0 / math.sqrt(2.0 * math.pi))
    return pre_act * normal_cdf, normal_cdf + pre_act * density


def swap(offset, size):
    return [(i, i ^ offset) for i in range(size)]


def per_device(
    tokens,
    doc_ids,
    norm1_gain,
    norm1_bias,
    norm2_gain,
    norm2_bias,
    w_qkv,
    b_qkv,
    w_out,
    b_out,
    w_up,
    b_up,
    w_down,
    b_down,
    cotangent,
):
    seq_rows, width_dev = tokens.shape
    n_row = lax.axis_size("row")
    n_col = lax.axis_size("col")
    width = width_dev * n_col
    rows_dev, heads_dev, triple = w_qkv.shape
    head_dim = triple // 3
    ff_dev = w_up.shape[1]
    pair = 2 if n_row % 2 == 0 and heads_dev % 2 == 0 and ff_dev % 2 == 0 else 1
    heads = heads_dev // pair
    ff = ff_dev // pair
    joint = heads * triple
    attn = heads * head_dim
    row = lax.axis_index("row")
    col = lax.axis_index("col")
    half = row % pair

    def exchange(halves):
        kept = halves[half]
        given = halves[pair - 1 - half]
        full = jnp.zeros((n_row,) + kept.shape, kept.dtype)
        full = lax.dynamic_update_slice(full, kept[None], (row, 0, 0))
        for offset in range(1, n_row):
            block = lax.ppermute(
                kept if offset % pair == 0 else given, "row", swap(offset, n_row)
            )
            full = lax.dynamic_update_slice(full, block[None], (row ^ offset, 0, 0))
        return full

    def split(w):
        return w.reshape(rows_dev, pair, -1).transpose(1, 0, 2)

    pack_one = jnp.concatenate([split(w_up), split(w_down.T)], axis=2)
    pack_two = jnp.concatenate([split(w_qkv.reshape(rows_dev, -1)), split(w_out.T)], axis=2)
    full_one = exchange(pack_one).reshape(width, 2 * ff)
    full_two = exchange(pack_two).reshape(width, joint + attn)
    w_up_full, w_down_full = full_one[:, :ff], full_one[:, ff:]
    w_qkv_full, w_out_full = full_two[:, :joint], full_two[:, joint:]

    def neighbours(x):
        return [x] + [lax.ppermute(x, "row", swap(1, n_row))] * (pair - 1)

    def gather(x):
        return lax.all_gather(x, "col", axis=1, tiled=True)

    affine = gather(jnp.stack([norm1_gain, norm1_bias, norm2_gain, norm2_bias]))
    token_rows = [gather(x) for x in neighbours(tokens)]
    grad_rows = [gather(x) for x in neighbours(cotangent)]
    docs = neighbours(doc_ids)

    bias_up = lax.dynamic_slice_in_dim(b_up.astype(F32), half * ff, ff)
    bias_qkv = lax.dynamic_slice_in_dim(b_qkv.astype(F32).reshape(-1), half * joint, joint)

    stats = []
    d_joints, d_pres, gelus, attns, outs = [], [], [], [], []
    sum_wd = jnp.zeros((width, ff), F32)
    ones, twos = [], []
    for x, dy, ids in zip(token_rows, grad_rows, docs):
        one, two, stat = normalize(x, affine)
        ones.append(one)
        twos.append(two)
        stats.append(stat)
        pre = jnp.dot(two, w_up_full, preferred_element_type=F32) + bias_up
        gelu, slope = gelu_slope(pre)
        gelu = gelu.astype(BF16)
        d_gelu = jnp.dot(dy, w_down_full, preferred_element_type=F32)
        d_pre = (d_gelu * slope).astype(BF16)
        qkv = jnp.dot(one, w_qkv_full, preferred_element_type=F32) + bias_qkv
        d_attn = jnp.dot(dy, w_out_full, preferred_element_type=F32).astype(BF16)
        starts = run_starts(ids)
        cos, sin = rotary_tables(jnp.arange(seq_rows, dtype=jnp.int32) - starts, head_dim)
        attended, d_joint = attention(qkv, d_attn, starts, cos, sin, head_dim)
        gelus.append(gelu)
        d_pres.append(d_pre)
        attns.append(attended)
        d_joints.append(d_joint)

    def over_tokens(lefts, rights):
        return functools.reduce(
            jnp.add,
            [
                lax.dot_general(a, b, TN, preferred_element_type=F32)
                for a, b in zip(lefts, rights)
            ],
        )

    grad_down = over_tokens(grad_rows, gelus)
    grad_up = over_tokens(twos, d_pres)
    grad_out = over_tokens(grad_rows, attns)
    grad_qkv = over_tokens(ones, d_joints)

    def reduce_rows(partial):
        blocks = partial.reshape(n_row, rows_dev, -1)
        kept = lax.dynamic_index_in_dim(blocks, row, 0, keepdims=False)
        given = None
        for offset in range(1, n_row):
            block = lax.dynamic_index_in_dim(blocks, row ^ offset, 0, keepdims=False)
            block = lax.ppermute(block.astype(BF16), "row", swap(offset, n_row)).astype(F32)
            if offset % pair == 0:
                kept = kept + block
            else:
                given = block if given is None else given + block
        if pair == 1:
            return kept[:, None]
        return jnp.where(
            half == 0, jnp.stack([kept, given], axis=1), jnp.stack([given, kept], axis=1)
        )

    def scatter(parts):
        shares = [
            lax.psum_scatter(p, "col", scatter_dimension=1, tiled=True) for p in parts
        ]
        total = shares[0].astype(F32)
        if pair > 1:
            total = total + lax.ppermute(shares[1], "row", swap(1, n_row)).astype(F32)
        return total

    branch = scatter(
        [
            (
                lax.dot_general(a, w_out_full, NT, preferred_element_type=F32)
                + lax.dot_general(g, w_down_full, NT, preferred_element_type=F32)
            ).astype(BF16)
            for a, g in zip(attns, gelus)
        ]
    )
    affine_wide = affine.astype(F32)
    back = scatter(
        [
            (
                lax.dot_general(dj, w_qkv_full, NT, preferred_element_type=F32) * affine_wide[0]
                + lax.dot_general(dp, w_up_full, NT, preferred_element_type=F32) * affine_wide[2]
            ).astype(BF16)
            for dj, dp in zip(d_joints, d_pres)
        ]
    )

    grad_w_down = reduce_rows(grad_down)
    grad_w_up = reduce_rows(grad_up)
    grad_w_out = reduce_rows(grad_out)
    grad_w_qkv = reduce_rows(grad_qkv)

    sum_joint = functools.reduce(jnp.add, [jnp.sum(d, 0, dtype=F32) for d in d_joints])
    sum_pre = functools.reduce(jnp.add, [jnp.sum(d, 0, dtype=F32) for d in d_pres])
    wide_qkv = w_qkv_full.astype(F32)
    wide_up = w_up_full.astype(F32)
    norm_sums = jnp.stack(
        [
            jnp.sum(wide_qkv * grad_qkv, 1),
            jnp.sum(wide_qkv * sum_joint, 1),
            jnp.sum(wide_up * grad_up, 1),
            jnp.sum(wide_up * sum_pre, 1),
        ]
    )
    norm_sums = lax.psum(norm_sums, ("row", "col"))
    norm_sums = lax.dynamic_slice_in_dim(norm_sums, col * width_dev, width_dev, axis=1)
    gain_one, shift_one = norm1_gain.astype(F32), norm1_bias.astype(F32)
    gain_two, shift_two = norm2_gain.astype(F32), norm2_bias.astype(F32)
    grad_gain_one = (norm_sums[0] - shift_one * norm_sums[1]) / gain_one
    grad_gain_two = (norm_sums[2] - shift_two * norm_sums[3]) / gain_two

    def place(v):
        return lax.dynamic_update_slice(jnp.zeros((pair * v.shape[0],), F32), v, (half * v.shape[0],))

    small = lax.psum(
        jnp.concatenate(
            [place(sum_joint), place(sum_pre), jnp.sum(grad_rows[0], 0, dtype=F32)]
        ),
        "row",
    )
    grad_b_qkv = small[: pair * joint].reshape(heads_dev, triple)
    grad_b_up = small[pair * joint : pair * (joint + ff)]
    grad_b_out = lax.dynamic_slice_in_dim(
        small[pair * (joint + ff) :], row * rows_dev, rows_dev
    )

    bias_out = lax.all_gather(
        jnp.stack([b_out, b_down]), "row", axis=1, tiled=True
    ).astype(F32)
    bias_out = lax.dynamic_slice_in_dim(bias_out[0] + bias_out[1], col * width_dev, width_dev)
    tokens_wide = tokens.astype(F32)
    layer_out = (tokens_wide + bias_out + branch).astype(BF16)

    mean, inv_std = stats[0][:, 0:1], stats[0][:, 1:2]
    normed = (tokens_wide - mean) * inv_std
    sums = lax.psum(jnp.stack([jnp.sum(back, 1), jnp.sum(back * normed, 1)]), "col") / width
    grad_tokens = cotangent.astype(F32) + inv_std * (
        back - sums[0][:, None] - normed * sums[1][:, None]
    )
    return (
        layer_out,
        grad_tokens,
        grad_gain_one,
        norm_sums[1],
        grad_gain_two,
        norm_sums[3],
        grad_w_qkv.reshape(rows_dev, heads_dev, triple),
        grad_b_qkv,
        grad_w_out.reshape(rows_dev, -1).T,
        grad_b_out,
        grad_w_up.reshape(rows_dev, -1),
        grad_b_up,
        grad_w_down.reshape(rows_dev, -1).T,
        grad_b_out,
    )


def solution(mesh):
    placed = (
        P("row", "col"),
        P("row"),
        P("col"),
        P("col"),
        P("col"),
        P("col"),
        P("row", "col", None),
        P("col", None),
        P("col", "row"),
        P("row"),
        P("row", "col"),
        P("col"),
        P("col", "row"),
        P("row"),
        P("row", "col"),
    )
    return jax.shard_map(
        per_device,
        mesh=mesh,
        in_specs=placed,
        out_specs=(
            P("row", "col"),
            P("row", "col"),
            P("col"),
            P("col"),
            P("col"),
            P("col"),
            P("row", "col", None),
            P("col", None),
            P("col", "row"),
            P("row"),
            P("row", "col"),
            P("col"),
            P("col", "row"),
            P("row"),
        ),
        check_vma=False,
    )
```

time: 1780 us -> 796 us (0.45)
  waiting for transfers between devices: 1160 us -> 203 us
  matrix products: 320 us -> 231 us
  other arithmetic: 128 us -> 42.4 us
  Pallas kernels: 0 us -> 70 us
  starting transfers between devices: 3.18 us -> 33.9 us
  blocking collectives: 94.2 us -> 122 us
  local copies, waits for them, and re-layouts: 53.2 us -> 73 us
    reduce_scatter x16 -> x4, waiting for transfers between devices: 855 us -> 0.03 us  [scatter(): lax.psum_scatter(p, 'col', scatter_dimension=1, tiled=True)]
    all_gather x16 -> x4, waiting for transfers between devices: 299 us -> 0.01 us  [gather(): return lax.all_gather(x, 'col', axis=1, tiled=True)]
    ppermute x0 -> x23, waiting for transfers between devices: none -> 202 us  [the longest x12 69.2 us: reduce_rows(): lax.ppermute(block.astype(BF16), 'row', swap(offset, n_row)).astype(F32)]
    dot_general x72 -> x24, matrix products: 320 us -> 231 us  [the longest x8 79.8 us: over_tokens(): lax.dot_general(a, b, TN, preferred_element_type=F32)]
    pallas_call x0 -> x4, Pallas kernels: none -> 70 us  [the longest x2 40.6 us: attention(): pl.pallas_call(functools.partial(attention_body, block, most, 1.0 / math....]
    convert_element_type x13 -> x2, other arithmetic: 62.6 us -> 0.15 us  [rotary_tables(): angles = inverse[:, None] * places.astype(F32)[None, :]]
    reduce_sum x23 -> x4, other arithmetic: 40.2 us -> 5.83 us  [the longest x1 2.36 us: per_device(): jnp.sum(back, 1)]
    ppermute x0 -> x23, starting transfers between devices: none -> 33.1 us  [the longest x12 14.4 us: reduce_rows(): lax.ppermute(block.astype(BF16), 'row', swap(offset, n_row)).astype(F32)]
  transfers between devices with their start and end apart: 33 -> 31, of which waited for: 23 -> 11; matrix products, arithmetic and copies ran while one was open for 27% -> 42% of each run, Pallas kernels for 0% -> 9%
where the time goes in v1:
time: 796 us; the launch traced here: 791 us
  matrix products  231 us (29%)
  waiting for transfers between devices  203 us (26%)
  blocking collectives  122 us (15%)
  local copies, waits for them, and re-layouts  73 us (9%)
  Pallas kernels  70 us (9%)
  other arithmetic  42.4 us (5%)
  starting transfers between devices  33.9 us (4%)
  between operations  15.4 us (2%)
    dot_general x8, matrix products, over_tokens(): lax.dot_general(a, b, TN, preferred_element_type=F32)  79.8 us
    ppermute x12, waiting for transfers between devices, reduce_rows(): lax.ppermute(block.astype(BF16), 'row', swap(offset, n_row)).astype(F32)  69.2 us
    ppermute x6, waiting for transfers between devices, exchange(): lax.ppermute(kept if offset % pair == 0 else given, 'row', swap(offset, n...  67.1 us
    ppermute x3, waiting for transfers between devices, neighbours(): return [x] + [lax.ppermute(x, 'row', swap(1, n_row))] * (pair - 1)  47 us
    pallas_call x2, Pallas kernels, attention(): pl.pallas_call(functools.partial(attention_body, block, most, 1.0 / math....  40.6 us
    psum x1, blocking collectives, per_device(): norm_sums = lax.psum(norm_sums, ('row', 'col'))  40.1 us
    all_gather x1, blocking collectives, per_device(): lax.all_gather(jnp.stack([b_out, b_down]), 'row', axis=1, tiled=True)  30.8 us
    pallas_call x2, Pallas kernels, normalize(): pl.pallas_call(norm_body, out_shape=(jax.ShapeDtypeStruct((length, width)...  29.3 us
  transfers between devices with their start and end apart: 31, of which 11 were waited for; matrix products, arithmetic and copies ran while one was open for 42% of the time, Pallas kernels for 9%

profile of v1, /device:TPU:0, one launch (start us, length us, event | category | flops | bytes accessed | tf_op | source)
XLA Modules:
  0.0 791.1 jit_solution(1391616716063696640)
XLA Ops:
  7.2 3.1 collective-permute-start.7
  10.3 23.4 %collective-permute-done.7 = bf16[2048,256]{1,0:T(8,128)(2,1)S(1)} collective-permute-done((bf16[2048,256]{1,0:T(8,128)(2,1)}, bf16[2048,256]{1,0:T(8,128)(2,1)S(1)}, u32[]{:S(2)}, u32[]{:S(2)}) %collective-permute-start.7) | collective-permute-done | bytes 1048608 | tf_op jit(solution)/shard_map/ppermute | solution.py:297
  36.5 22.8 %collective-permute-done.8 = bf16[2048,256]{1,0:T(8,128)(2,1)S(1)} collective-permute-done((bf16[2048,256]{1,0:T(8,128)(2,1)}, bf16[2048,256]{1,0:T(8,128)(2,1)S(1)}, u32[]{:S(2)}, u32[]{:S(2)}) %collective-permute-start.8) | collective-permute-done | bytes 1048608 | tf_op jit(solution)/shard_map/ppermute | solution.py:297
  63.4 3.4 collective-permute-start.2
  70.1 2.3 copy.88
  72.5 2.5 broadcast_in_dim.53
  76.8 2.9 collective-permute-start.4
  79.9 9.1 %all_gather.20.affine_ref = bf16[4,2048]{1,0:T(4,128)(2,1)S(1)} all-gather(bf16[4,256]{1,0:T(4,128)(2,1)S(1)} %pad_maximum_fusion.4), channel_id=1, replica_groups=mesh['row'=4,'col'=8] {'col'}, dimensions={1}, use_global_device_ids=true | all-gather | bytes 18432 | tf_op jit(solution)/shard_map/all_gather | solution.py:300
  90.8 2.5 collective-permute-start.3
  94.1 7.3 multiply_sine_fusion.1
  107.4 26.7 %collective-permute-done.1 = bf16[512,512]{1,0:T(8,128)(2,1)} collective-permute-done((bf16[512,512]{1,0:T(8,128)(2,1)}, bf16[512,512]{1,0:T(8,128)(2,1)}, u32[]{:S(2)}, u32[]{:S(2)}) %collective-permute-start.1) | collective-permute-done | bytes 524320 | tf_op jit(solution)/shard_map/ppermute | solution.py:280
  136.3 10.9 %collective-permute-done.3 = bf16[512,1024]{1,0:T(8,128)(2,1)} collective-permute-done((bf16[512,1024]{1,0:T(8,128)(2,1)}, bf16[512,1024]{1,0:T(8,128)(2,1)}, u32[]{:S(2)}, u32[]{:S(2)}) %collective-permute-start.3) | collective-permute-done | bytes 1048608 | tf_op jit(solution)/shard_map/ppermute | solution.py:280
  147.1 2.3 bitcast_dynamic-update-slice_fusion.2
  149.4 29.5 %collective-permute-done.4 = bf16[512,1024]{1,0:T(8,128)(2,1)S(1)} collective-permute-done((bf16[512,1024]{1,0:T(8,128)(2,1)}, bf16[512,1024]{1,0:T(8,128)(2,1)S(1)}, u32[]{:S(2)}, u32[]{:S(2)}) %collective-permute-start.4) | collective-permute-done | bytes 1048608 | tf_op jit(solution)/shard_map/ppermute | solution.py:280
  181.0 14.5 %normalize.3 = (bf16[2048,2048]{1,0:T(8,128)(2,1)}, bf16[2048,2048]{1,0:T(8,128)(2,1)}, f32[2048,2]{1,0:T(8,128)}) custom-call(bf16[2048,2048]{1,0:T(8,128)(2,1)} %all-gather.9.cloned.1.call-done.x_ref, bf16[4,2048]{1,0:T(4,128)(2,1)} %copy-done.16), custom_call_target="tpu_custom_call" | custom-call | flops 41943040 | bytes 25165824 | tf_op jit(solution)/shard_map/normalize/pallas_call | solution.py:213
  195.5 6.7 fusion.18.grad_ref
  202.2 6.1 convolution_add_fusion.2.q_ref.k_ref.v_ref
  208.4 20.0 %attention.3 = (bf16[2048,128]{1,0:T(8,128)(2,1)}, bf16[2048,384]{1,0:T(8,128)(2,1)}) custom-call(s32[8]{0:T(128)} %and_select_fusion.low_ref, s32[1,2048]{1,0:T(1,128)} %bitcast.220, f32[2048,384]{1,0:T(8,128)} %convolution_add_fusion.2.q_ref.k_ref.v_ref, f32[2048,384]{1,0:T(8,128)} %convolution_add_fusion.2.q_ref.k_ref.v_ref, ...), custom_call_target="tpu_custom_call" | custom-call | flops 2013265920 | bytes 6291456 | tf_op jit(solution)/shard_map/attention/pallas_call | solution.py:152
  228.4 10.0 %fusion.48 = f32[2048,2048]{1,0:T(8,128)} fusion(bf16[2048,384]{1,0:T(8,128)(2,1)} %get-tuple-element.31, bf16[2048,512]{1,0:T(8,128)(2,1)S(1)} %bitcast.195), kind=kOutput, calls=%fused_computation.116 | convolution fusion | flops 3221225472 | bytes 19922944 | tf_op jit(solution)/shard_map/dot_general | solution.py:387
  238.5 6.4 fusion.43
  244.9 8.6 %convert_reduce_fusion.1 = (f32[512]{0:T(512)S(1)}, bf16[2048,512]{1,0:T(8,128)(2,1)S(1)}) fusion(f32[2048,512]{1,0:T(8,128)S(1)} %fusion.43, f32[512]{0:T(512)S(1)} %dynamic_slice.87, bf16[2048,2048]{1,0:T(8,128)(2,1)S(1)} %bitcast.188, bf16[2048,1024]{1,0:T(8,128)(2,1)} %bitcast.24), kind=kOutput, calls=%fused_computation.24 | convolution fusion | flops 4308598272 | bytes 16781312 | tf_op jit(solution)/shard_map/dot_general | solution.py:322
  254.8 11.1 %add_convert_fusion = bf16[2048,2048]{1,0:T(8,128)(2,1)} fusion(f32[2048,2048]{1,0:T(8,128)} %fusion.48, bf16[2048,512]{1,0:T(8,128)(2,1)S(1)} %get-tuple-element.133, f32[2048]{0:T(1024)S(1)} %bitcast.227, f32[2048]{0:T(1024)S(1)} %bitcast.225, bf16[2048,1024]{1,0:T(8,128)(2,1)} %bitcast.24), kind=kOutput, calls=%fused_computation.1 | convolution fusion | flops 4311744512 | bytes 29376512 | tf_op jit(solution)/shard_map/dot_general | solution.py:388
  266.2 13.2 %fusion.32 = f32[2048,2048]{1,0:T(8,128)} fusion(bf16[2048,1024]{1,0:T(8,128)(2,1)} %bitcast.24, f32[2048,512]{1,0:T(8,128)} %copy-done.1, f32[512]{0:T(512)S(1)} %dynamic_slice.87), kind=kOutput, calls=%fused_computation.73 | convolution fusion | flops 4301258752 | bytes 23070720 | tf_op jit(solution)/shard_map/dot_general | solution.py:378
  279.5 11.6 %add_convert_fusion.2 = bf16[2048,2048]{1,0:T(8,128)(2,1)} fusion(f32[2048,2048]{1,0:T(8,128)} %fusion.32, bf16[2048,128]{1,0:T(8,128)(2,1)S(1)} %copy-done.8, bf16[2048,512]{1,0:T(8,128)(2,1)S(1)} %bitcast.196), kind=kOutput, calls=%fused_computation.3 | convolution fusion | flops 1082130432 | bytes 26214400 | tf_op jit(solution)/shard_map/dot_general | solution.py:377
  292.0 14.9 %normalize.2 = (bf16[2048,2048]{1,0:T(8,128)(2,1)}, bf16[2048,2048]{1,0:T(8,128)(2,1)}, f32[2048,2]{1,0:T(8,128)}) custom-call(bf16[2048,2048]{1,0:T(8,128)(2,1)} %all-gather.5.cloned.1.call-done.x_ref, bf16[4,2048]{1,0:T(4,128)(2,1)} %copy-done.16), custom_call_target="tpu_custom_call" | custom-call | flops 41943040 | bytes 25165824 | tf_op jit(solution)/shard_map/normalize/pallas_call | solution.py:213
  306.9 7.1 fusion.17.grad_ref
  313.9 6.3 convolution_add_fusion.3.q_ref.k_ref.v_ref
  320.2 20.6 %attention.2 = (bf16[2048,128]{1,0:T(8,128)(2,1)}, bf16[2048,384]{1,0:T(8,128)(2,1)}) custom-call(s32[8]{0:T(128)} %and_select_fusion.1.low_ref, s32[1,2048]{1,0:T(1,128)} %bitcast.218, f32[2048,384]{1,0:T(8,128)} %convolution_add_fusion.3.q_ref.k_ref.v_ref, f32[2048,384]{1,0:T(8,128)} %convolution_add_fusion.3.q_ref.k_ref.v_ref, ...), custom_call_target="tpu_custom_call" | custom-call | flops 2013265920 | bytes 6291456 | tf_op jit(solution)/shard_map/attention/pallas_call | solution.py:152
  340.8 10.3 %fusion.50 = f32[2048,2048]{1,0:T(8,128)} fusion(bf16[2048,384]{1,0:T(8,128)(2,1)} %get-tuple-element.30, bf16[2048,512]{1,0:T(8,128)(2,1)S(1)} %bitcast.199), kind=kOutput, calls=%fused_computation.118 | convolution fusion | flops 3221225472 | bytes 19922944 | tf_op jit(solution)/shard_map/dot_general | solution.py:387
  351.1 6.3 fusion.45
  357.5 8.6 %convert_reduce_fusion.2 = (f32[512]{0:T(512)S(1)}, bf16[2048,512]{1,0:T(8,128)(2,1)S(1)}) fusion(f32[2048,512]{1,0:T(8,128)S(1)} %fusion.45, f32[512]{0:T(512)S(1)} %dynamic_slice.87, bf16[2048,2048]{1,0:T(8,128)(2,1)S(1)} %bitcast.190, bf16[2048,1024]{1,0:T(8,128)(2,1)} %bitcast.24), kind=kOutput, calls=%fused_computation.25 | convolution fusion | flops 4308598272 | bytes 16781312 | tf_op jit(solution)/shard_map/dot_general | solution.py:322
  367.4 13.9 %add_convert_fusion.1 = bf16[2048,2048]{1,0:T(8,128)(2,1)} fusion(f32[2048,2048]{1,0:T(8,128)} %fusion.50, bf16[2048,512]{1,0:T(8,128)(2,1)S(1)} %get-tuple-element.131, f32[2048]{0:T(1024)S(1)} %bitcast.228, f32[2048]{0:T(1024)S(1)} %bitcast.226, bf16[2048,1024]{1,0:T(8,128)(2,1)} %bitcast.24), kind=kOutput, calls=%fused_computation.2 | convolution fusion | flops 4311744512 | bytes 29376512 | tf_op jit(solution)/shard_map/dot_general | solution.py:388
  382.1 30.8 %all_gather.18 = bf16[2,2048]{1,0:T(2,128)(2,1)S(1)} all-gather(bf16[2,512]{1,0:T(2,128)(2,1)S(1)} %pad_maximum_fusion.3), channel_id=1, replica_groups=mesh['row'=4,'col'=8] {'row'}, dimensions={1}, use_global_device_ids=true | all-gather | bytes 10240 | tf_op jit(solution)/shard_map/all_gather | solution.py:433
  416.1 13.5 %fusion.34 = f32[2048,2048]{1,0:T(8,128)} fusion(bf16[2048,1024]{1,0:T(8,128)(2,1)} %bitcast.24, f32[2048,512]{1,0:T(8,128)} %copy-done.44, f32[512]{0:T(512)S(1)} %dynamic_slice.87), kind=kOutput, calls=%fused_computation.75 | convolution fusion | flops 4301258752 | bytes 23070720 | tf_op jit(solution)/shard_map/dot_general | solution.py:378
  429.6 11.7 %add_convert_fusion.3 = bf16[2048,2048]{1,0:T(8,128)(2,1)} fusion(f32[2048,2048]{1,0:T(8,128)} %fusion.34, bf16[2048,128]{1,0:T(8,128)(2,1)S(1)} %copy-done.9, bf16[2048,512]{1,0:T(8,128)(2,1)S(1)} %bitcast.200), kind=kOutput, calls=%fused_computation.4 | convolution fusion | flops 1082130432 | bytes 26214400 | tf_op jit(solution)/shard_map/dot_general | solution.py:377
  441.3 12.0 %fusion.82 = f32[2048,384]{1,0:T(8,128)} fusion(bf16[2048,2048]{1,0:T(8,128)(2,1)} %get-tuple-element.23, bf16[2048,384]{1,0:T(8,128)(2,1)} %get-tuple-element.30), kind=kOutput, calls=%fused_computation.203 | convolution fusion | flops 3221225472 | bytes 13107200 | tf_op jit(solution)/shard_map/dot_general | solution.py:338
  453.3 10.1 %fusion.83 = f32[2048,512]{1,0:T(8,128)} fusion(bf16[2048,2048]{1,0:T(8,128)(2,1)} %get-tuple-element.25, bf16[2048,512]{1,0:T(8,128)(2,1)S(1)} %copy-done.48), kind=kOutput, calls=%fused_computation.204 | convolution fusion | flops 4294967296 | bytes 14680064 | tf_op jit(solution)/shard_map/dot_general | solution.py:338
  463.5 6.0 fusion.84
  469.5 10.0 %fusion.75 = f32[512,2048]{1,0:T(8,128)} fusion(bf16[2048,2048]{1,0:T(8,128)(2,1)} %all-gather.7.cloned.1.call-done, f32[2048,512]{1,0:T(8,128)S(1)} %copy-done.45, f32[512]{0:T(512)S(1)} %dynamic_slice.87), kind=kOutput, calls=%fused_computation.196 | convolution fusion | flops 4301258752 | bytes 16779264 | tf_op jit(solution)/shard_map/dot_general | solution.py:338
  482.6 18.0 %psum.23 = f32[3840]{0:T(1024)S(1)} all-reduce(f32[3840]{0:T(1024)S(1)} %pad_maximum_fusion.2), channel_id=1, replica_groups=mesh['row'=4,'col'=8] {'row'}, use_global_device_ids=true, to_apply=%region_21.22 | all-reduce | flops 3840 | bytes 30720 | tf_op jit(solution)/shard_map/psum | solution.py:421
  502.4 5.2 fusion.16
  509.2 2.8 constant_dynamic-slice_fusion.7
  515.6 4.2 collective-permute-start.14
  519.8 12.6 %fusion.14 = (f32[2048]{0:T(1024)}, f32[2048]{0:T(1024)}, f32[2048,384]{1,0:T(8,128)S(1)}) fusion(bf16[2048,512]{1,0:T(8,128)(2,1)S(1)} %bitcast.201, f32[384]{0:T(512)} %get-tuple-element.83, f32[2048,384]{1,0:T(8,128)} %fusion.82, bf16[2048,2048]{1,0:T(8,128)(2,1)} %get-tuple-element.26, bf16[2048,384]{1,0:T(8,128)(2,1)} %get-tuple-element.31), kind=kOutput, calls=%fused_computation.32 | convolution fusion | flops 3225939968 | bytes 17843712 | tf_op jit(solution)/shard_map/dot_general | solution.py:338
  535.7 2.4 collective-permute-start.13
  538.1 10.6 %add_bitcast_fusion = f32[2048,512]{0,1:T(8,128)} fusion(f32[512,2048]{1,0:T(8,128)S(1)} %copy-done.7, bf16[2048,2048]{1,0:T(8,128)(2,1)} %all-gather.11.cloned.1.call-done, f32[2048,512]{1,0:T(8,128)S(1)} %copy-done.2, f32[512]{0:T(512)S(1)} %copy-done.22), kind=kOutput, calls=%fused_computation.23 | convolution fusion | flops 4302307328 | bytes 20973568 | tf_op jit(solution)/shard_map/dot_general | solution.py:338
  548.7 6.0 reshape.226
  556.7 8.4 %constant_dynamic-slice_fusion.3 = (bf16[1,512,512]{1,0,2:T(2,128)(2,1)S(1)}, bf16[1,512,512]{1,0,2:T(2,128)(2,1)}, bf16[1,512,512]{1,0,2:T(2,128)(2,1)S(1)}) fusion(f32[4,512,512]{1,0,2:T(4,128)} %reshape.226, s32[]{:T(128)S(6)} %select_n.130, s32[]{:T(128)S(6)} %select_n.129, s32[]{:T(128)S(6)} %select_n.131), kind=kLoop, calls=%fused_computation.156 | loop fusion | bytes 3145740 | tf_op jit(solution)/shard_map/jit(dynamic_index_in_dim)/dynamic_slice | solution.py:353
  565.1 2.3 copy.112
  567.4 3.1 constant_dynamic-slice_fusion.4
  571.8 3.5 copy.113
  577.6 13.2 %fusion = (f32[2048]{0:T(1024)S(1)}, f32[2048]{0:T(1024)S(1)}, f32[2048,512]{1,0:T(8,128)}) fusion(bf16[2048,1024]{1,0:T(8,128)(2,1)} %bitcast.24, f32[512]{0:T(512)} %get-tuple-element.85, f32[2048,512]{1,0:T(8,128)} %fusion.83, bf16[2048,2048]{1,0:T(8,128)(2,1)} %get-tuple-element.28, bf16[2048,512]{1,0:T(8,128)(2,1)} %copy-done.46), kind=kOutput, calls=%fused_computation.9 | convolution fusion | flops 4301254656 | bytes 20989952 | tf_op jit(solution)/shard_map/dot_general | solution.py:338
  590.8 40.1 %psum.22 = f32[4,2048]{1,0:T(4,128)S(1)} all-reduce(f32[4,2048]{1,0:T(4,128)S(1)} %pad_maximum_fusion), channel_id=1, replica_groups=mesh['row'=4,'col'=8] {'row','col'}, use_global_device_ids=true, to_apply=%region_19.20 | all-reduce | flops 8192 | bytes 65536 | tf_op jit(solution)/shard_map/psum | solution.py:411
  632.2 3.1 fusion.54
  641.7 2.3 collective-permute-start.20
  644.0 13.3 %collective-permute-done.12 = bf16[512,384]{1,0:T(8,128)(2,1)} collective-permute-done((bf16[512,384]{1,0:T(8,128)(2,1)S(1)}, bf16[512,384]{1,0:T(8,128)(2,1)}, u32[]{:S(2)}, u32[]{:S(2)}) %collective-permute-start.12) | collective-permute-done | bytes 393248 | tf_op jit(solution)/shard_map/ppermute | solution.py:354
  661.4 2.4 copy.104
  663.7 45.4 %collective-permute-done.20 = bf16[512,512]{1,0:T(8,128)(2,1)S(1)} collective-permute-done((bf16[512,512]{1,0:T(8,128)(2,1)S(1)}, bf16[512,512]{1,0:T(8,128)(2,1)S(1)}, u32[]{:S(2)}, u32[]{:S(2)}) %collective-permute-start.20) | collective-permute-done | bytes 524320 | tf_op jit(solution)/shard_map/ppermute | solution.py:354
  717.4 3.0 collective-permute-done.17
  721.9 7.5 collective-permute-done.18
  733.1 18.7 %collective-permute-done.10 = bf16[2048,256]{1,0:T(8,128)(2,1)S(1)} collective-permute-done((bf16[2048,256]{1,0:T(8,128)(2,1)}, bf16[2048,256]{1,0:T(8,128)(2,1)S(1)}, u32[]{:S(2)}, u32[]{:S(2)}) %collective-permute-start.10) | collective-permute-done | bytes 1048608 | tf_op jit(solution)/shard_map/ppermute | solution.py:371
  751.8 2.4 fusion.29
  754.2 24.0 %psum.21 = f32[2,2048]{1,0:T(2,128)S(1)} all-reduce(f32[2,2048]{1,0:T(2,128)S(1)} %pad_maximum_fusion.1), channel_id=1, replica_groups=mesh['row'=4,'col'=8] {'col'}, use_global_device_ids=true, to_apply=%region_10.11 | all-reduce | flops 4096 | bytes 32768 | tf_op jit(solution)/shard_map/psum | solution.py:442
  778.3 5.1 fusion.27
  (271 shorter events, 77.3 us)
Async XLA Ops:
  7.2 54.6 %copy-start.17 = (bf16[256,512]{1,0:T(8,128)(2,1)S(1)}, bf16[256,512]{1,0:T(8,128)(2,1)}, u32[]{:S(2)}) copy-start(bf16[256,512]{1,0:T(8,128)(2,1)} %param.23) | copy-start | bytes 786436
  7.2 54.7 %copy-start.13 = (bf16[512,2,384]{2,1,0:T(2,128)(2,1)S(1)}, bf16[512,2,384]{2,1,0:T(2,128)(2,1)}, u32[]{:S(2)}) copy-start(bf16[512,2,384]{2,1,0:T(2,128)(2,1)} %param.21) | copy-start | bytes 2359300
  7.2 173.8 %all-gather.9.cloned.1.call-start = ((), (), s32[]{:S(2)}) async-start(), calls=%async_computation.7 | async-start | bytes 9437184 | tf_op jit(solution)/shard_map/all_gather | solution.py:300
  7.2 26.5 %collective-permute-start.7 = (bf16[2048,256]{1,0:T(8,128)(2,1)}, bf16[2048,256]{1,0:T(8,128)(2,1)S(1)}, u32[]{:S(2)}, u32[]{:S(2)}) collective-permute-start(bf16[2048,256]{1,0:T(8,128)(2,1)} %param.15), channel_id=1, source_target_pairs={{0,8},{8,0},{16,24},{24,16},{1,9},{9,1},{17,25},{25,17},{2,10},{10... | collective-permute-start | bytes 3145736 | tf_op jit(solution)/shard_map/ppermute | solution.py:297
  34.7 160.8 %all-gather.11.cloned.1.call-start = ((), (), s32[]{:S(2)}) async-start(), calls=%async_computation.8 | async-start | bytes 9437184 | tf_op jit(solution)/shard_map/all_gather | solution.py:300
  34.7 24.6 %collective-permute-start.8 = (bf16[2048,256]{1,0:T(8,128)(2,1)}, bf16[2048,256]{1,0:T(8,128)(2,1)S(1)}, u32[]{:S(2)}, u32[]{:S(2)}) collective-permute-start(bf16[2048,256]{1,0:T(8,128)(2,1)} %param.29), channel_id=1, source_target_pairs={{0,8},{8,0},{16,24},{24,16},{1,9},{9,1},{17,25},{25,17},{2,10},{10... | collective-permute-start | bytes 3145736 | tf_op jit(solution)/shard_map/ppermute | solution.py:297
  60.4 231.7 %all-gather.5.cloned.1.call-start = ((), (), s32[]{:S(2)}) async-start(), calls=%async_computation.4 | async-start | bytes 9437184 | tf_op jit(solution)/shard_map/all_gather | solution.py:300
  61.1 245.8 %all-gather.7.cloned.1.call-start = ((), (), s32[]{:S(2)}) async-start(), calls=%async_computation.5 | async-start | bytes 9437184 | tf_op jit(solution)/shard_map/all_gather | solution.py:300
  61.7 648.5 %reduce-scatter.11.cloned.1.call-start = ((), (), s32[]{:S(2)}) async-start(), calls=%async_computation.11 | async-start | bytes 9437184 | tf_op jit(solution)/shard_map/reduce_scatter | solution.py:367
  63.4 71.8 %collective-permute-start.2 = (bf16[512,512]{1,0:T(8,128)(2,1)}, bf16[512,512]{1,0:T(8,128)(2,1)}, u32[]{:S(2)}, u32[]{:S(2)}) collective-permute-start(bf16[512,512]{1,0:T(8,128)(2,1)} %get-tuple-element.108), channel_id=1, source_target_pairs={{0,24},{8,16},{16,8},{24,0},{1,25},{9,17},{17,9},{25,1},{2,26},{10... | collective-permute-start | bytes 1572872 | tf_op jit(solution)/shard_map/ppermute | solution.py:280
  66.8 39.1 %collective-permute-start = (bf16[512,512]{1,0:T(8,128)(2,1)}, bf16[512,512]{1,0:T(8,128)(2,1)}, u32[]{:S(2)}, u32[]{:S(2)}) collective-permute-start(bf16[512,512]{1,0:T(8,128)(2,1)} %get-tuple-element.108), channel_id=1, source_target_pairs={{0,8},{8,0},{16,24},{24,16},{1,9},{9,1},{17,25},{25,17},{2,10},{10... | collective-permute-start | bytes 1572872 | tf_op jit(solution)/shard_map/ppermute | solution.py:280
  66.8 24.0 %collective-permute-start.6 = (s32[2048]{0:T(1024)S(1)}, s32[2048]{0:T(1024)S(1)}, u32[]{:S(2)}, u32[]{:S(2)}) collective-permute-start(s32[2048]{0:T(1024)S(1)} %copy-done.20), channel_id=1, source_target_pairs={{0,8},{8,0},{16,24},{24,16},{1,9},{9,1},{17,25},{25,17},{2,10},{10... | collective-permute-start | bytes 24584 | tf_op jit(solution)/shard_map/ppermute | solution.py:297
  68.8 65.3 %collective-permute-start.1 = (bf16[512,512]{1,0:T(8,128)(2,1)}, bf16[512,512]{1,0:T(8,128)(2,1)}, u32[]{:S(2)}, u32[]{:S(2)}) collective-permute-start(bf16[512,512]{1,0:T(8,128)(2,1)} %get-tuple-element.107), channel_id=1, source_target_pairs={{0,16},{8,24},{16,0},{24,8},{1,17},{9,25},{17,1},{25,9},{2,18},{10... | collective-permute-start | bytes 1572872 | tf_op jit(solution)/shard_map/ppermute | solution.py:280
  72.4 16.9 %copy-start.31 = (bf16[2,384]{1,0:T(2,128)(2,1)S(1)}, bf16[2,384]{1,0:T(2,128)(2,1)}, u32[]{:S(2)}) copy-start(bf16[2,384]{1,0:T(2,128)(2,1)} %param.22) | copy-start | bytes 4612
  72.5 17.3 %copy-start.30 = (bf16[1024]{0:T(1024)(128)(2,1)S(1)}, bf16[1024]{0:T(1024)(128)(2,1)}, u32[]{:S(2)}) copy-start(bf16[1024]{0:T(1024)(128)(2,1)} %param.26) | copy-start | bytes 6148
  76.8 102.1 %collective-permute-start.4 = (bf16[512,1024]{1,0:T(8,128)(2,1)}, bf16[512,1024]{1,0:T(8,128)(2,1)S(1)}, u32[]{:S(2)}, u32[]{:S(2)}) collective-permute-start(bf16[512,1024]{1,0:T(8,128)(2,1)} %get-tuple-element.99), channel_id=1, source_target_pairs={{0,16},{8,24},{16,0},{24,8},{1,17},{9,25},{17,1},{25,9},{2,18},{10... | collective-permute-start | bytes 3145736 | tf_op jit(solution)/shard_map/ppermute | solution.py:280
  89.0 14.4 %copy-start.16 = (bf16[4,2048]{1,0:T(4,128)(2,1)}, bf16[4,2048]{1,0:T(4,128)(2,1)S(1)}, u32[]{:S(2)}) copy-start(bf16[4,2048]{1,0:T(4,128)(2,1)S(1)} %all_gather.20.affine_ref) | copy-start | bytes 49156
  89.9 379.6 %copy-start.21 = (f32[512]{0:T(512)}, f32[512]{0:T(512)S(1)}, u32[]{:S(2)}) copy-start(f32[512]{0:T(512)S(1)} %dynamic_slice.87) | copy-start | bytes 6148
  90.8 56.3 %collective-permute-start.3 = (bf16[512,1024]{1,0:T(8,128)(2,1)}, bf16[512,1024]{1,0:T(8,128)(2,1)}, u32[]{:S(2)}, u32[]{:S(2)}) collective-permute-start(bf16[512,1024]{1,0:T(8,128)(2,1)} %get-tuple-element.100), channel_id=1, source_target_pairs={{0,8},{8,0},{16,24},{24,16},{1,9},{9,1},{17,25},{25,17},{2,10},{10... | collective-permute-start | bytes 3145736 | tf_op jit(solution)/shard_map/ppermute | solution.py:280
  94.0 11.2 %copy-start.19 = (s32[16,128]{1,0:T(8,128)}, s32[16,128]{1,0:T(8,128)S(1)}, u32[]{:S(2)}) copy-start(s32[16,128]{1,0:T(8,128)S(1)} %get-tuple-element.89) | copy-start | bytes 24580
  94.1 197.3 %copy-start.18 = (s32[16,128]{1,0:T(8,128)}, s32[16,128]{1,0:T(8,128)S(1)}, u32[]{:S(2)}) copy-start(s32[16,128]{1,0:T(8,128)S(1)} %get-tuple-element.87) | copy-start | bytes 24580
  105.9 74.1 %collective-permute-start.5 = (bf16[512,1024]{1,0:T(8,128)(2,1)}, bf16[512,1024]{1,0:T(8,128)(2,1)S(1)}, u32[]{:S(2)}, u32[]{:S(2)}) collective-permute-start(bf16[512,1024]{1,0:T(8,128)(2,1)} %get-tuple-element.100), channel_id=1, source_target_pairs={{0,24},{8,16},{16,8},{24,0},{1,25},{9,17},{17,9},{25,1},{2,26},{10... | collective-permute-start | bytes 3145736 | tf_op jit(solution)/shard_map/ppermute | solution.py:280
  208.4 30.1 %slice-start.6 = ((s8[8388608]{0:T(1024)(128)(4,1)}), s8[4194304]{0:T(1024)(128)(4,1)S(1)}, s32[]{:S(2)}) async-start(s8[8388608]{0:T(1024)(128)(4,1)} %bitcast.240), calls=%async_computation.18 | async-start | bytes 8388608
  228.4 16.5 %slice-start = ((s8[8388608]{0:T(1024)(128)(4,1)}), s8[4194304]{0:T(1024)(128)(4,1)S(1)}, s32[]{:S(2)}) async-start(s8[8388608]{0:T(1024)(128)(4,1)} %bitcast.187), calls=%async_computation.12 | async-start | bytes 8388608
  266.0 13.5 %copy-start.8 = (bf16[2048,128]{1,0:T(8,128)(2,1)S(1)}, bf16[2048,128]{1,0:T(8,128)(2,1)}, u32[]{:S(2)}) copy-start(bf16[2048,128]{1,0:T(8,128)(2,1)} %get-tuple-element.27) | copy-start | bytes 1572868
  266.0 466.6 %reduce-scatter.7.cloned.1.call-start = ((), (), s32[]{:S(2)}) async-start(), calls=%async_computation.9 | async-start | bytes 9437184 | tf_op jit(solution)/shard_map/reduce_scatter | solution.py:367
  291.1 442.0 %reduce-scatter.9.cloned.1.call-start = ((), (), s32[]{:S(2)}) async-start(), calls=%async_computation.10 | async-start | bytes 9437184 | tf_op jit(solution)/shard_map/reduce_scatter | solution.py:367
  320.2 30.9 %slice-start.8 = ((s8[8388608]{0:T(1024)(128)(4,1)}), s8[4194304]{0:T(1024)(128)(4,1)S(1)}, s32[]{:S(2)}) async-start(s8[8388608]{0:T(1024)(128)(4,1)} %bitcast.242), calls=%async_computation.20 | async-start | bytes 8388608
  340.8 16.7 %slice-start.2 = ((s8[8388608]{0:T(1024)(128)(4,1)}), s8[4194304]{0:T(1024)(128)(4,1)S(1)}, s32[]{:S(2)}) async-start(s8[8388608]{0:T(1024)(128)(4,1)} %bitcast.189), calls=%async_computation.14 | async-start | bytes 8388608
  381.4 32.1 %copy-start.5 = (f32[2048,2]{1,0:T(8,128)S(1)}, f32[2048,2]{1,0:T(8,128)}, u32[]{:S(2)}) copy-start(f32[2048,2]{1,0:T(8,128)} %get-tuple-element.29) | copy-start | bytes 49156
  381.4 396.8 %reduce-scatter.5.cloned.1.call-start = ((), (), s32[]{:S(2)}) async-start(), calls=%async_computation.6 | async-start | bytes 9437184 | tf_op jit(solution)/shard_map/reduce_scatter | solution.py:367
  416.1 13.5 %copy-start.9 = (bf16[2048,128]{1,0:T(8,128)(2,1)S(1)}, bf16[2048,128]{1,0:T(8,128)(2,1)}, u32[]{:S(2)}) copy-start(bf16[2048,128]{1,0:T(8,128)(2,1)} %get-tuple-element.24) | copy-start | bytes 1572868
  441.3 12.0 %copy-start.48 = (bf16[2048,512]{1,0:T(8,128)(2,1)S(1)}, bf16[2048,512]{1,0:T(8,128)(2,1)}, u32[]{:S(2)}) copy-start(bf16[2048,512]{1,0:T(8,128)(2,1)} %copy-done.47) | copy-start | bytes 6291460
  463.5 16.1 %slice-start.4 = ((s8[8388608]{0:T(1024)(128)(4,1)}), s8[4194304]{0:T(1024)(128)(4,1)S(1)}, s32[]{:S(2)}) async-start(s8[8388608]{0:T(1024)(128)(4,1)} %bitcast.191), calls=%async_computation.16 | async-start | bytes 8388608
  515.4 122.1 %collective-permute-start.16 = (bf16[512,128]{1,0:T(8,128)(2,1)}, bf16[512,128]{1,0:T(8,128)(2,1)}, u32[]{:S(2)}, u32[]{:S(2)}) collective-permute-start(bf16[512,128]{1,0:T(8,128)(2,1)} %bitcast.153), channel_id=1, source_target_pairs={{0,24},{8,16},{16,8},{24,0},{1,25},{9,17},{17,9},{25,1},{2,26},{10... | collective-permute-start | bytes 393224 | tf_op jit(solution)/shard_map/ppermute | solution.py:354
  515.4 124.2 %collective-permute-start.15 = (bf16[512,128]{1,0:T(8,128)(2,1)S(1)}, bf16[512,128]{1,0:T(8,128)(2,1)}, u32[]{:S(2)}, u32[]{:S(2)}) collective-permute-start(bf16[512,128]{1,0:T(8,128)(2,1)S(1)} %bitcast.216), channel_id=1, source_target_pairs={{0,8},{8,0},{16,24},{24,16},{1,9},{9,1},{17,25},{25,17},{2,10},{10... | collective-permute-start | bytes 393224 | tf_op jit(solution)/shard_map/ppermute | solution.py:354
  515.6 119.7 %collective-permute-start.14 = (bf16[512,128]{1,0:T(8,128)(2,1)}, bf16[512,128]{1,0:T(8,128)(2,1)}, u32[]{:S(2)}, u32[]{:S(2)}) collective-permute-start(bf16[512,128]{1,0:T(8,128)(2,1)} %bitcast.155), channel_id=1, source_target_pairs={{0,16},{8,24},{16,0},{24,8},{1,17},{9,25},{17,1},{25,9},{2,18},{10... | collective-permute-start | bytes 393224 | tf_op jit(solution)/shard_map/ppermute | solution.py:354
  519.8 18.3 %copy-start.2 = (f32[2048,512]{1,0:T(8,128)S(1)}, f32[2048,512]{1,0:T(8,128)}, u32[]{:S(2)}) copy-start(f32[2048,512]{1,0:T(8,128)} %copy-done.1) | copy-start | bytes 12582916
  519.8 18.3 %copy-start.7 = (f32[512,2048]{1,0:T(8,128)S(1)}, f32[512,2048]{1,0:T(8,128)}, u32[]{:S(2)}) copy-start(f32[512,2048]{1,0:T(8,128)} %fusion.75) | copy-start | bytes 12582916
  519.8 18.3 %copy-start.22 = (f32[512]{0:T(512)S(1)}, f32[512]{0:T(512)}, u32[]{:S(2)}) copy-start(f32[512]{0:T(512)} %copy-done.21) | copy-start | bytes 6148
  535.2 123.2 %collective-permute-start.11 = (bf16[512,384]{1,0:T(8,128)(2,1)}, bf16[512,384]{1,0:T(8,128)(2,1)}, u32[]{:S(2)}, u32[]{:S(2)}) collective-permute-start(bf16[512,384]{1,0:T(8,128)(2,1)} %get-tuple-element.96), channel_id=1, source_target_pairs={{0,16},{8,24},{16,0},{24,8},{1,17},{9,25},{17,1},{25,9},{2,18},{10... | collective-permute-start | bytes 1179656 | tf_op jit(solution)/shard_map/ppermute | solution.py:354
  535.7 106.0 %collective-permute-start.13 = (bf16[512,384]{1,0:T(8,128)(2,1)}, bf16[512,384]{1,0:T(8,128)(2,1)}, u32[]{:S(2)}, u32[]{:S(2)}) collective-permute-start(bf16[512,384]{1,0:T(8,128)(2,1)} %get-tuple-element.97), channel_id=1, source_target_pairs={{0,24},{8,16},{16,8},{24,0},{1,25},{9,17},{17,9},{25,1},{2,26},{10... | collective-permute-start | bytes 1179656 | tf_op jit(solution)/shard_map/ppermute | solution.py:354
  577.6 13.2 %copy-start.25 = (f32[2048]{0:T(1024)S(1)}, f32[2048]{0:T(1024)}, u32[]{:S(2)}) copy-start(f32[2048]{0:T(1024)} %get-tuple-element.76) | copy-start | bytes 24580
  577.6 13.2 %copy-start.26 = (f32[2048]{0:T(1024)S(1)}, f32[2048]{0:T(1024)}, u32[]{:S(2)}) copy-start(f32[2048]{0:T(1024)} %get-tuple-element.77) | copy-start | bytes 24580
  577.6 53.5 %copy-start.35 = (bf16[256]{0:T(256)(128)(2,1)S(1)}, bf16[256]{0:T(256)(128)(2,1)}, u32[]{:S(2)}) copy-start(bf16[256]{0:T(256)(128)(2,1)} %param.20) | copy-start | bytes 1540
  577.6 53.5 %copy-start.37 = (bf16[256]{0:T(256)(128)(2,1)S(1)}, bf16[256]{0:T(256)(128)(2,1)}, u32[]{:S(2)}) copy-start(bf16[256]{0:T(256)(128)(2,1)} %param.19) | copy-start | bytes 1540
  577.6 54.1 %copy-start.39 = (bf16[256]{0:T(256)(128)(2,1)S(1)}, bf16[256]{0:T(256)(128)(2,1)}, u32[]{:S(2)}) copy-start(bf16[256]{0:T(256)(128)(2,1)} %param.18) | copy-start | bytes 1540
  577.6 54.1 %copy-start.41 = (bf16[256]{0:T(256)(128)(2,1)S(1)}, bf16[256]{0:T(256)(128)(2,1)}, u32[]{:S(2)}) copy-start(bf16[256]{0:T(256)(128)(2,1)} %param.17) | copy-start | bytes 1540
  577.6 57.7 %copy-start.15 = (bf16[512,384]{1,0:T(8,128)(2,1)S(1)}, bf16[512,384]{1,0:T(8,128)(2,1)}, u32[]{:S(2)}) copy-start(bf16[512,384]{1,0:T(8,128)(2,1)} %get-tuple-element.98) | copy-start | bytes 1179652
  590.8 50.9 %copy-start.14 = (bf16[1,512,512]{2,1,0:T(8,128)(2,1)S(1)}, bf16[1,512,512]{2,1,0:T(8,128)(2,1)}, u32[]{:S(2)}) copy-start(bf16[1,512,512]{2,1,0:T(8,128)(2,1)} %copy.112) | copy-start | bytes 1572868
  631.0 28.9 %copy-start.28 = (f32[1,256]{1,0:T(1,128)}, f32[1,256]{1,0:T(1,128)S(1)}, u32[]{:S(2)}) copy-start(f32[1,256]{1,0:T(1,128)S(1)} %get-tuple-element.110) | copy-start | bytes 3076
  631.0 28.9 %copy-start.29 = (f32[1,256]{1,0:T(1,128)}, f32[1,256]{1,0:T(1,128)S(1)}, u32[]{:S(2)}) copy-start(f32[1,256]{1,0:T(1,128)S(1)} %get-tuple-element.112) | copy-start | bytes 3076
  635.3 22.0 %collective-permute-start.12 = (bf16[512,384]{1,0:T(8,128)(2,1)S(1)}, bf16[512,384]{1,0:T(8,128)(2,1)}, u32[]{:S(2)}, u32[]{:S(2)}) collective-permute-start(bf16[512,384]{1,0:T(8,128)(2,1)S(1)} %copy-done.15), channel_id=1, source_target_pairs={{0,8},{8,0},{16,24},{24,16},{1,9},{9,1},{17,25},{25,17},{2,10},{10... | collective-permute-start | bytes 1179656 | tf_op jit(solution)/shard_map/ppermute | solution.py:354
  637.5 72.7 %collective-permute-start.22 = (bf16[512,512]{1,0:T(8,128)(2,1)}, bf16[512,512]{1,0:T(8,128)(2,1)}, u32[]{:S(2)}, u32[]{:S(2)}) collective-permute-start(bf16[512,512]{1,0:T(8,128)(2,1)} %bitcast.150), channel_id=1, source_target_pairs={{0,24},{8,16},{16,8},{24,0},{1,25},{9,17},{17,9},{25,1},{2,26},{10... | collective-permute-start | bytes 1572872 | tf_op jit(solution)/shard_map/ppermute | solution.py:354
  639.6 72.6 %collective-permute-start.21 = (bf16[512,512]{1,0:T(8,128)(2,1)}, bf16[512,512]{1,0:T(8,128)(2,1)}, u32[]{:S(2)}, u32[]{:S(2)}) collective-permute-start(bf16[512,512]{1,0:T(8,128)(2,1)} %bitcast.151), channel_id=1, source_target_pairs={{0,8},{8,0},{16,24},{24,16},{1,9},{9,1},{17,25},{25,17},{2,10},{10... | collective-permute-start | bytes 1572872 | tf_op jit(solution)/shard_map/ppermute | solution.py:354
  641.7 67.4 %collective-permute-start.20 = (bf16[512,512]{1,0:T(8,128)(2,1)S(1)}, bf16[512,512]{1,0:T(8,128)(2,1)S(1)}, u32[]{:S(2)}, u32[]{:S(2)}) collective-permute-start(bf16[512,512]{1,0:T(8,128)(2,1)S(1)} %bitcast.213), channel_id=1, source_target_pairs={{0,16},{8,24},{16,0},{24,8},{1,17},{9,25},{17,1},{25,9},{2,18},{10... | collective-permute-start | bytes 1572872 | tf_op jit(solution)/shard_map/ppermute | solution.py:354
  657.3 63.1 %collective-permute-start.17 = (bf16[512,512]{1,0:T(8,128)(2,1)}, bf16[512,512]{1,0:T(8,128)(2,1)}, u32[]{:S(2)}, u32[]{:S(2)}) collective-permute-start(bf16[512,512]{1,0:T(8,128)(2,1)} %get-tuple-element.93), channel_id=1, source_target_pairs={{0,16},{8,24},{16,0},{24,8},{1,17},{9,25},{17,1},{25,9},{2,18},{10... | collective-permute-start | bytes 1572872 | tf_op jit(solution)/shard_map/ppermute | solution.py:354
  658.5 63.4 %collective-permute-start.19 = (bf16[512,512]{1,0:T(8,128)(2,1)}, bf16[512,512]{1,0:T(8,128)(2,1)}, u32[]{:S(2)}, u32[]{:S(2)}) collective-permute-start(bf16[512,512]{1,0:T(8,128)(2,1)} %get-tuple-element.94), channel_id=1, source_target_pairs={{0,24},{8,16},{16,8},{24,0},{1,25},{9,17},{17,9},{25,1},{2,26},{10... | collective-permute-start | bytes 1572872 | tf_op jit(solution)/shard_map/ppermute | solution.py:354
  709.1 20.3 %collective-permute-start.18 = (bf16[512,512]{1,0:T(8,128)(2,1)}, bf16[512,512]{1,0:T(8,128)(2,1)}, u32[]{:S(2)}, u32[]{:S(2)}) collective-permute-start(bf16[512,512]{1,0:T(8,128)(2,1)} %get-tuple-element.95), channel_id=1, source_target_pairs={{0,8},{8,0},{16,24},{24,16},{1,9},{9,1},{17,25},{25,17},{2,10},{10... | collective-permute-start | bytes 1572872 | tf_op jit(solution)/shard_map/ppermute | solution.py:354
  710.2 41.6 %collective-permute-start.10 = (bf16[2048,256]{1,0:T(8,128)(2,1)}, bf16[2048,256]{1,0:T(8,128)(2,1)S(1)}, u32[]{:S(2)}, u32[]{:S(2)}) collective-permute-start(bf16[2048,256]{1,0:T(8,128)(2,1)} %reduce-scatter.11.cloned.1.call-done), channel_id=1, source_target_pairs={{0,8},{8,0},{16,24},{24,16},{1,9},{9,1},{17,25},{25,17},{2,10},{10... | collective-permute-start | bytes 3145736 | tf_op jit(solution)/shard_map/ppermute | solution.py:371
  730.8 21.0 %copy-start = (bf16[2048,256]{1,0:T(8,128)(2,1)S(1)}, bf16[2048,256]{1,0:T(8,128)(2,1)}, u32[]{:S(2)}) copy-start(bf16[2048,256]{1,0:T(8,128)(2,1)} %param.15) | copy-start | bytes 3145732
  731.1 47.2 %copy-start.4 = (bf16[2048,256]{1,0:T(8,128)(2,1)S(1)}, bf16[2048,256]{1,0:T(8,128)(2,1)}, u32[]{:S(2)}) copy-start(bf16[2048,256]{1,0:T(8,128)(2,1)} %param.29) | copy-start | bytes 3145732
  731.1 47.2 %copy-start.27 = (f32[1,256]{1,0:T(1,128)S(1)}, f32[1,256]{1,0:T(1,128)}, u32[]{:S(2)}) copy-start(f32[1,256]{1,0:T(1,128)} %fusion.72) | copy-start | bytes 3076
  732.6 45.6 %collective-permute-start.9 = (bf16[2048,256]{1,0:T(8,128)(2,1)}, bf16[2048,256]{1,0:T(8,128)(2,1)}, u32[]{:S(2)}, u32[]{:S(2)}) collective-permute-start(bf16[2048,256]{1,0:T(8,128)(2,1)} %reduce-scatter.7.cloned.1.call-done), channel_id=1, source_target_pairs={{0,8},{8,0},{16,24},{24,16},{1,9},{9,1},{17,25},{25,17},{2,10},{10... | collective-permute-start | bytes 3145736 | tf_op jit(solution)/shard_map/ppermute | solution.py:371
  (26 other events, 138.3 us)
Sparse Core Ops, SparseCore 0:
  34.8 57.4 all-gather.8
  94.8 55.9 all-gather.10
  152.6 55.9 all-gather.4
  210.3 55.9 all-gather.6
  269.6 86.4 reduce-scatter.10
  359.9 71.2 reduce-scatter.6
  434.6 71.2 reduce-scatter.8
  509.8 71.2 reduce-scatter.4
